TPU v7x, 1024 devices: a whole 4x8x16 slice. The times are simulated.
1024 devices in a mesh: section: 8 (over x, core), expert: 32 (over z, y_lo), dp: 4 (over y_hi).
Axes of the slice: x: 4, y: 8 (y_hi: 4, y_lo: 2; y = y_hi * 2 + y_lo), z: 16, core: 2. Of those that a mesh axis runs over, the one named last changes fastest.
Arguments:
- panel: bfloat16 [12288, 4096], P(('section', 'expert', 'dp')), may hold values from -6 to 6
- norm_gain: float32 [4096], replicated, may hold values from 0.5 to 1.5
- expert_ids: int32 [12288, 8], P(('section', 'expert', 'dp')), may hold values from 0 to 63, all different within a row; in each aligned block of 12 rows (0 to 11, 12 to 23, ...) at most 2 rows name the same one
- gate_scores: float32 [12288, 8], P(('section', 'expert', 'dp')), may hold values from 0.05 to 1
- w_gate: bfloat16 [64, 4096, 768], P('expert', 'dp'), may hold values from -0.09375 to 0.09375
- w_up: bfloat16 [64, 4096, 768], P('expert', 'dp'), may hold values from -0.09375 to 0.09375
- w_down: bfloat16 [64, 768, 4096], P('expert', None, 'dp'), may hold values from -0.21875 to 0.21875
Outputs:
- mixed_out: bfloat16 [12288, 4096], P(('section', 'expert', 'dp'))
Inputs may be any that keep to these rules, and one draw needn't show every extreme that they name: `expert_ids`: each row names 8 different experts. In each aligned block of 12 rows (the rows of one device) no expert is named by more than 2 rows, a bound that some block reaches.
All inputs are finite; a program needn't handle non-finite values.
Results may differ from a plain program's by a relative error of at most 0.008.
Values may be sent and summed in bfloat16 or wider, within the bound.
A program may use at most 64 MiB of HBM per device.

v0:
```python
import jax
import jax.numpy as jnp
from jax import lax
from jax.sharding import PartitionSpec as P

CAP = 2


def passed_along(shard, axis, by):
    peers = lax.axis_size(axis)
    return lax.ppermute(shard, axis, [(i, (i + by) % peers) for i in range(peers)])


def per_device(panel, norm_gain, expert_ids, gate_scores, w_gate, w_up, w_down):
    arrived = passed_along(panel, "section", 1)
    arrived_f = arrived.astype(jnp.float32)
    mean_sq = jnp.mean(arrived_f * arrived_f, axis=-1, keepdims=True)
    normed = (arrived_f * lax.rsqrt(mean_sq + 1e-06) * norm_gain).astype(jnp.bfloat16)
    experts_here = w_gate.shape[0]
    width_part = w_gate.shape[1]
    expert_groups = lax.axis_size("expert")
    dp_groups = lax.axis_size("dp")
    tokens_here = expert_ids.shape[0]
    top_k = expert_ids.shape[1]
    slot_rows = experts_here * CAP
    all_slots = expert_groups * slot_rows
    flat_ids = expert_ids.reshape(-1)
    expert_hits = (
        flat_ids[:, None] == jnp.arange(expert_groups * experts_here, dtype=jnp.int32)[None, :]
    ).astype(jnp.int32)
    earlier = jnp.cumsum(expert_hits, axis=0) - expert_hits
    slot_index = jnp.sum(earlier * expert_hits, axis=1)
    target = flat_ids * CAP + slot_index
    placed = (target[:, None] == jnp.arange(all_slots, dtype=jnp.int32)[None, :]).reshape(
        tokens_here, top_k, all_slots
    )
    occupied = jnp.any(placed, axis=1).astype(jnp.bfloat16)
    send_rows = jnp.einsum(
        "ts,td->sd", occupied, normed, preferred_element_type=jnp.float32
    ).astype(jnp.bfloat16)
    outgoing = send_rows.reshape(1, expert_groups, slot_rows, send_rows.shape[1])
    incoming = lax.all_to_all(
        lax.all_to_all(outgoing, "expert", split_axis=1, concat_axis=1, tiled=True),
        "dp",
        split_axis=3,
        concat_axis=0,
        tiled=True,
    )
    grouped = incoming.reshape(dp_groups, expert_groups, experts_here, CAP, width_part)
    gate_part = jnp.einsum("abecd,edf->abecf", grouped, w_gate, preferred_element_type=jnp.float32)
    up_part = jnp.einsum("abecd,edf->abecf", grouped, w_up, preferred_element_type=jnp.float32)
    gate_full, up_full = (
        lax.psum(gate_part.astype(jnp.bfloat16), "dp").astype(jnp.float32),
        lax.psum(up_part.astype(jnp.bfloat16), "dp").astype(jnp.float32),
    )
    hidden = (jax.nn.silu(gate_full) * up_full).astype(jnp.bfloat16)
    expert_out = jnp.einsum(
        "abecf,efd->abecd", hidden, w_down, preferred_element_type=jnp.float32
    ).astype(jnp.bfloat16)
    returning = expert_out.reshape(dp_groups, expert_groups, slot_rows, width_part)
    returned = lax.all_to_all(
        lax.all_to_all(returning, "expert", split_axis=1, concat_axis=1, tiled=True),
        "dp",
        split_axis=0,
        concat_axis=3,
        tiled=True,
    )
    back_rows = returned.reshape(all_slots, returned.shape[3])
    weights = (gate_scores / jnp.sum(gate_scores, axis=-1, keepdims=True)).astype(jnp.bfloat16)
    combine = jnp.sum(
        jnp.where(placed, weights[:, :, None].astype(jnp.float32), 0.0), axis=1
    ).astype(jnp.bfloat16)
    mixed_out = arrived_f + jnp.dot(combine, back_rows, preferred_element_type=jnp.float32)
    return mixed_out.astype(jnp.bfloat16)


def solution(mesh):
    in_specs = (
        P(("section", "expert", "dp"), None),
        P(),
        P(("section", "expert", "dp"), None),
        P(("section", "expert", "dp"), None),
        P("expert", "dp", None),
        P("expert", "dp", None),
        P("expert", None, "dp"),
    )
    out_specs = P(("section", "expert", "dp"), None)
    return jax.shard_map(
        per_device, mesh=mesh, in_specs=in_specs, out_specs=out_specs, check_vma=False
    )
```

profile of v0, /device:TPU:8, one launch (start us, length us, event | category | flops | bytes accessed | tf_op | source)
XLA Modules:
  0.0 357.4 jit_solution(14562854424898786979)
XLA Ops:
  6.5 0.0 copy-start
  6.5 0.0 all-reduce.3.cloned.1.call-start
  6.5 0.0 collective-permute-start
  6.5 0.9 copy.51
  7.5 0.1 eq.29
  7.5 0.1 fusion.41
  7.6 0.1 reduce_window_sum.11
  7.8 0.2 select_reduce_fusion.1
  8.0 0.1 reduce_sum.39
  8.0 0.1 fusion.40
  8.2 4.2 %collective-permute-done = bf16[12,4096]{1,0:T(8,128)(2,1)S(1)} collective-permute-done((bf16[12,4096]{1,0:T(8,128)(2,1)}, bf16[12,4096]{1,0:T(8,128)(2,1)S(1)}, u32[]{:S(2)}, u32[]{:S(2)}) %collective-permute-start) | collective-permute-done | bytes 98336 | tf_op jit(solution)/shard_map/ppermute | solution.py:11
  12.4 0.1 fusion.34
  12.5 2.2 convolution_convert_fusion
  14.8 2.3 reshape.45
  17.0 72.9 %all_to_all.40 = bf16[1,32,4,4096]{3,2,0,1:T(4,128)(2,1)} all-to-all(bf16[1,32,4,4096]{3,2,0,1:T(4,128)(2,1)} %bitcast.53), channel_id=1, replica_groups=mesh['section'=8,'expert'=32,'dp'=4] {'expert'}, dimensions={1} | all-to-all | bytes 2097152 | tf_op jit(solution)/shard_map/all_to_all | solution.py:43
  89.9 7.2 %copy.55 = bf16[1,32,4,4096]{1,2,0,3:T(4,128)(2,1)} copy(bf16[1,32,4,4096]{3,2,0,1:T(4,128)(2,1)} %all_to_all.40) | data formatting | bytes 2097152 | tf_op jit(solution)/shard_map/all_to_all | solution.py:43
  97.2 6.4 %reshape.52 = bf16[4,2,65536]{2,1,0:T(2,128)(2,1)} reshape(bf16[4096,1,4,32]{3,2,1,0:T(4,128)(2,1)} %bitcast.49) | data formatting | bytes 2097152
  103.6 25.6 %all_to_all.41 = bf16[4,2,65536]{2,1,0:T(2,128)(2,1)} all-to-all(bf16[4,2,65536]{2,1,0:T(2,128)(2,1)} %reshape.52), channel_id=1, replica_groups=mesh['section'=8,'expert'=32,'dp'=4] {'dp'}, dimensions={0} | all-to-all | bytes 2097152 | tf_op jit(solution)/shard_map/all_to_all | solution.py:42
  129.2 5.0 %reshape.53 = bf16[4096,1,4,32]{3,2,1,0:T(4,128)(2,1)} reshape(bf16[4,2,65536]{2,1,0:T(2,128)(2,1)} %all_to_all.41) | data formatting | bytes 2097152
  134.3 7.2 %copy.67 = bf16[1,32,4,4,1024]{4,3,1,2,0:T(4,128)(2,1)} copy(bf16[1,32,4,4,1024]{1,2,4,3,0:T(4,128)(2,1)} %bitcast.50) | data formatting | bytes 2097152 | tf_op jit(solution)/shard_map/all_to_all | solution.py:42
  141.5 1.5 copy.57
  143.0 0.0 copy-start.2
  143.0 3.9 %fusion.24 = bf16[4,32,2,2,768]{4,1,3,0,2:T(8,128)(2,1)} fusion(bf16[2,1024,768]{2,1,0:T(8,128)(2,1)} %param.12, bf16[4,32,2,2,1024]{4,1,3,2,0:T(8,128)(2,1)S(1)} %bitcast.56), kind=kOutput, calls=%fused_computation.20 | convolution fusion | flops 805699584 | bytes 4980736 | tf_op jit(solution)/shard_map/abecd,edf->abecf/dot_general | solution.py:51
  147.0 0.0 copy-done.2
  147.0 1.9 fusion.27
  148.9 0.0 all-reduce.3.cloned.1.call-update
  148.9 91.1 %all-reduce.3.cloned.1.call-done = (bf16[4,32,2,2,768]{4,1,3,0,2:T(8,128)(2,1)}, bf16[4,32,2,2,768]{4,1,3,0,2:T(8,128)(2,1)}) async-done(((bf16[4,32,2,2,768]{4,1,3,0,2:T(8,128)(2,1)}, bf16[4,32,2,2,768]{4,1,3,0,2:T(8,128)(2,1)}), (bf16[4,32,2,2,768]{4,1,3,0,2:T(8,128)(2,1)}, bf16[4,32,2,2,768]{4,1,3,0,2:T(8,128)(2,1)})) %all-reduce.3.cloned.1.call-update) | async-done | bytes 1572880 | tf_op jit(solution)/shard_map/psum | solution.py:54
  240.0 0.0 copy-done
  240.0 2.5 fusion.21
  242.5 0.1 copy.60
  242.6 0.8 copy.61
  243.4 0.0 copy-start.1
  243.4 70.6 %all_to_all.42 = bf16[4,32,4,1024]{3,2,0,1:T(4,128)(2,1)S(1)} all-to-all(bf16[4,32,4,1024]{3,2,0,1:T(4,128)(2,1)S(1)} %copy.61), channel_id=1, replica_groups=mesh['section'=8,'expert'=32,'dp'=4] {'expert'}, dimensions={1} | all-to-all | bytes 2097152 | tf_op jit(solution)/shard_map/all_to_all | solution.py:62
  313.9 1.4 copy.62
  315.4 4.7 %all-to-all-start.3 = ((bf16[4,32,4,1024]{3,2,1,0:T(4,128)(2,1)}), bf16[4,32,4,1024]{3,2,1,0:T(4,128)(2,1)}, u32[]{:S(2)}, u32[]{:S(2)}) async-start(bf16[4,32,4,1024]{3,2,1,0:T(4,128)(2,1)} %copy.62), calls=%async_computation.3 | async-start | bytes 2097152 | tf_op jit(solution)/shard_map/all_to_all | solution.py:61
  320.0 0.0 copy-done.1
  320.1 0.1 copy.53
  320.1 0.1 select_reduce_fusion
  320.3 27.0 %all-to-all-done.3 = bf16[4,32,4,1024]{3,2,1,0:T(4,128)(2,1)} async-done(((bf16[4,32,4,1024]{3,2,1,0:T(4,128)(2,1)}), bf16[4,32,4,1024]{3,2,1,0:T(4,128)(2,1)}, u32[]{:S(2)}, u32[]{:S(2)}) %all-to-all-start.3) | async-done | bytes 1048608 | tf_op jit(solution)/shard_map/all_to_all | solution.py:61
  347.3 2.0 copy.63
  349.3 0.4 copy.68
  349.7 0.9 fusion
  (4 shorter events, 0.0 us)
Async XLA Ops:
  6.5 233.5 %copy-start = (bf16[2,768,1024]{2,1,0:T(8,128)(2,1)S(1)}, bf16[2,768,1024]{2,1,0:T(8,128)(2,1)}, u32[]{:S(2)}) copy-start(bf16[2,768,1024]{2,1,0:T(8,128)(2,1)} %param.13) | copy-start | bytes 9437188
  6.5 233.4 %all-reduce.3.cloned.1.call-start = ((), (), s32[]{:S(2)}) async-start(), calls=%async_computation.4 | async-start | bytes 3145728 | tf_op jit(solution)/shard_map/psum | solution.py:54
  6.5 5.8 %collective-permute-start = (bf16[12,4096]{1,0:T(8,128)(2,1)}, bf16[12,4096]{1,0:T(8,128)(2,1)S(1)}, u32[]{:S(2)}, u32[]{:S(2)}) collective-permute-start(bf16[12,4096]{1,0:T(8,128)(2,1)} %param.7), channel_id=1, source_target_pairs={{0,128},{128,256},{256,384},{384,512},{512,640},{640,768},{768,896... | collective-permute-start | bytes 294920 | tf_op jit(solution)/shard_map/ppermute | solution.py:11
  143.0 3.9 %copy-start.2 = (bf16[2,1024,768]{2,1,0:T(8,128)(2,1)S(1)}, bf16[2,1024,768]{2,1,0:T(8,128)(2,1)}, u32[]{:S(2)}) copy-start(bf16[2,1024,768]{2,1,0:T(8,128)(2,1)} %param.11) | copy-start | bytes 9437188
  243.4 76.7 %copy-start.1 = (f32[12,8]{0,1:T(8,128)S(1)}, f32[12,8]{0,1:T(8,128)}, u32[]{:S(2)}) copy-start(f32[12,8]{0,1:T(8,128)} %param.10) | copy-start | bytes 1156
  315.4 31.9 %all-to-all-start.3 = ((bf16[4,32,4,1024]{3,2,1,0:T(4,128)(2,1)}), bf16[4,32,4,1024]{3,2,1,0:T(4,128)(2,1)}, u32[]{:S(2)}, u32[]{:S(2)}) async-start(bf16[4,32,4,1024]{3,2,1,0:T(4,128)(2,1)} %copy.62), calls=%async_computation.3 | async-start | bytes 2097152 | tf_op jit(solution)/shard_map/all_to_all | solution.py:61
Sparse Core Ops, SparseCore 0:
  149.0 90.9 all-reduce.2
where the time goes:
time: 358 us; the launch traced here: 357 us
  blocking collectives  169 us (47%)
  waiting for transfers between devices  122 us (34%)
  local copies, waits for them, and re-layouts  35.6 us (10%)
  between operations  13.5 us (4%)
  matrix products  11.4 us (3%)
  starting transfers between devices  4.67 us (1%)
    psum x1, waiting for transfers between devices, per_device(): lax.psum(up_part.astype(jnp.bfloat16), 'dp').astype(jnp.float32)  91.1 us
    all_to_all x1, blocking collectives, per_device(): lax.all_to_all(outgoing, 'expert', split_axis=1, concat_axis=1, tiled=True)  72.9 us
    all_to_all x1, blocking collectives, per_device(): lax.all_to_all(returning, 'expert', split_axis=1, concat_axis=1, tiled=True)  70.6 us
    all_to_all x1, waiting for transfers between devices, per_device(): lax.all_to_all(lax.all_to_all(returning, 'expert', split_axis=1, concat_a...  27 us
    all_to_all x1, blocking collectives, per_device(): lax.all_to_all(lax.all_to_all(outgoing, 'expert', split_axis=1, concat_ax...  25.6 us
    unnamed x10, local copies, waits for them, and re-layouts  12.8 us
    all_to_all x2, local copies, waits for them, and re-layouts, per_device(): lax.all_to_all(lax.all_to_all(outgoing, 'expert', split_axis=1, concat_ax...  8.75 us
    all_to_all x1, local copies, waits for them, and re-layouts, per_device(): lax.all_to_all(outgoing, 'expert', split_axis=1, concat_axis=1, tiled=True)  7.24 us
  transfers between devices with their start and end apart: 3, of which 3 were waited for; matrix products, arithmetic and copies ran while one was open for 1% of the time, Pallas kernels for 0%

commit v1 on v0

--- a/solution.py
+++ b/solution.py
@@ -34,43 +34,40 @@
     placed = (target[:, None] == jnp.arange(all_slots, dtype=jnp.int32)[None, :]).reshape(
         tokens_here, top_k, all_slots
     )
-    occupied = jnp.any(placed, axis=1).astype(jnp.bfloat16)
+    occupied = jnp.any(placed, axis=1).astype(jnp.bfloat16).reshape(
+        tokens_here, expert_groups, slot_rows
+    )
+    normed_parts = normed.reshape(tokens_here, dp_groups, width_part)
     send_rows = jnp.einsum(
-        "ts,td->sd", occupied, normed, preferred_element_type=jnp.float32
+        "tes,tpw->epsw", occupied, normed_parts, preferred_element_type=jnp.float32
     ).astype(jnp.bfloat16)
-    outgoing = send_rows.reshape(1, expert_groups, slot_rows, send_rows.shape[1])
+    devices = expert_groups * dp_groups
+    outgoing = send_rows.reshape(devices, slot_rows, width_part)
     incoming = lax.all_to_all(
-        lax.all_to_all(outgoing, "expert", split_axis=1, concat_axis=1, tiled=True),
-        "dp",
-        split_axis=3,
-        concat_axis=0,
-        tiled=True,
+        outgoing, ("expert", "dp"), split_axis=0, concat_axis=0, tiled=True
     )
-    grouped = incoming.reshape(dp_groups, expert_groups, experts_here, CAP, width_part)
-    gate_part = jnp.einsum("abecd,edf->abecf", grouped, w_gate, preferred_element_type=jnp.float32)
-    up_part = jnp.einsum("abecd,edf->abecf", grouped, w_up, preferred_element_type=jnp.float32)
+    grouped = incoming.reshape(devices, experts_here, CAP, width_part)
+    gate_part = jnp.einsum("nxcd,xdf->nxcf", grouped, w_gate, preferred_element_type=jnp.float32)
+    up_part = jnp.einsum("nxcd,xdf->nxcf", grouped, w_up, preferred_element_type=jnp.float32)
     gate_full, up_full = (
         lax.psum(gate_part.astype(jnp.bfloat16), "dp").astype(jnp.float32),
         lax.psum(up_part.astype(jnp.bfloat16), "dp").astype(jnp.float32),
     )
     hidden = (jax.nn.silu(gate_full) * up_full).astype(jnp.bfloat16)
     expert_out = jnp.einsum(
-        "abecf,efd->abecd", hidden, w_down, preferred_element_type=jnp.float32
+        "nxcf,xfd->nxcd", hidden, w_down, preferred_element_type=jnp.float32
     ).astype(jnp.bfloat16)
-    returning = expert_out.reshape(dp_groups, expert_groups, slot_rows, width_part)
+    returning = expert_out.reshape(devices, slot_rows, width_part)
     returned = lax.all_to_all(
-        lax.all_to_all(returning, "expert", split_axis=1, concat_axis=1, tiled=True),
-        "dp",
-        split_axis=0,
-        concat_axis=3,
-        tiled=True,
+        returning, ("expert", "dp"), split_axis=0, concat_axis=0, tiled=True
     )
-    back_rows = returned.reshape(all_slots, returned.shape[3])
+    back = returned.reshape(expert_groups, dp_groups, slot_rows, width_part)
     weights = (gate_scores / jnp.sum(gate_scores, axis=-1, keepdims=True)).astype(jnp.bfloat16)
     combine = jnp.sum(
         jnp.where(placed, weights[:, :, None].astype(jnp.float32), 0.0), axis=1
-    ).astype(jnp.bfloat16)
-    mixed_out = arrived_f + jnp.dot(combine, back_rows, preferred_element_type=jnp.float32)
+    ).astype(jnp.bfloat16).reshape(tokens_here, expert_groups, slot_rows)
+    mixed = jnp.einsum("tes,epsw->tpw", combine, back, preferred_element_type=jnp.float32)
+    mixed_out = arrived_f + mixed.reshape(tokens_here, dp_groups * width_part)
     return mixed_out.astype(jnp.bfloat16)
 
 

time: 358 us -> 279 us (0.78)
  the two profiles are of different devices: /device:TPU:8 before, /device:TPU:26 now
where the time goes in v1:
time: 279 us
  waiting for transfers between devices  146 us (52%)
  blocking collectives  81.1 us (29%)
  starting transfers between devices  18 us (6%)
  between operations  13.5 us (5%)
  local copies, waits for them, and re-layouts  10 us (4%)
  matrix products  8.91 us (3%)
    psum x1, waiting for transfers between devices, per_device(): lax.psum(up_part.astype(jnp.bfloat16), 'dp').astype(jnp.float32)  87.8 us
    all_to_all x1, blocking collectives, per_device(): lax.all_to_all(outgoing, ('expert', 'dp'), split_axis=0, concat_axis=0, t...  81.1 us
    all_to_all x1, waiting for transfers between devices, per_device(): lax.all_to_all(returning, ('expert', 'dp'), split_axis=0, concat_axis=0,...  55.1 us
    all_to_all x1, starting transfers between devices, per_device(): lax.all_to_all(returning, ('expert', 'dp'), split_axis=0, concat_axis=0,...  18 us
  transfers between devices with their start and end apart: 3, of which 3 were waited for; matrix products, arithmetic and copies ran while one was open for 1% of the time, Pallas kernels for 0%

profile of v1, /device:TPU:26, one launch (start us, length us, event | category | flops | bytes accessed | tf_op | source)
XLA Modules:
  0.0 278.8 jit_solution(15903083917699807894)
XLA Ops:
  6.5 0.0 copy-start
  6.5 0.0 all-reduce.3.cloned.1.call-start
  6.5 0.0 collective-permute-start
  6.5 0.9 copy.30
  7.5 0.1 eq.29
  7.5 0.1 fusion.36
  7.6 0.1 reduce_window_sum.11
  7.8 0.2 select_reduce_fusion.1
  8.0 0.1 reduce_sum.39
  8.0 0.1 fusion.35
  8.2 0.1 copy.34
  8.3 0.1 copy.36
  8.4 2.7 collective-permute-done
  11.1 0.1 fusion.31
  11.3 0.8 fusion.33
  12.1 0.1 reshape.60
  12.2 0.5 fusion.22
  12.7 0.8 copy.37
  13.5 0.0 copy-start.2
  13.5 81.1 %all_to_all.10 = bf16[128,4,1024]{2,1,0:T(4,128)(2,1)S(1)} all-to-all(bf16[128,4,1024]{2,1,0:T(4,128)(2,1)S(1)} %bitcast.57), channel_id=1, replica_groups=mesh['section'=8,'expert'=32,'dp'=4] {'expert','dp'}, dimensions={0} | all-to-all | bytes 2097152 | tf_op jit(solution)/shard_map/all_to_all | solution.py:46
  94.6 0.3 copy.38
  94.9 0.0 copy-done.2
  94.9 0.0 copy-start.3
  94.9 1.9 fusion.23
  96.8 0.0 copy-done.3
  96.8 1.9 fusion.26
  98.7 0.0 all-reduce.3.cloned.1.call-update
  98.7 87.8 %all-reduce.3.cloned.1.call-done = (bf16[128,2,2,768]{3,0,2,1:T(8,128)(2,1)}, bf16[128,2,2,768]{3,0,2,1:T(8,128)(2,1)}) async-done(((bf16[128,2,2,768]{3,0,2,1:T(8,128)(2,1)}, bf16[128,2,2,768]{3,0,2,1:T(8,128)(2,1)}), (bf16[128,2,2,768]{3,0,2,1:T(8,128)(2,1)}, bf16[128,2,2,768]{3,0,2,1:T(8,128)(2,1)})) %all-reduce.3.cloned.1.call-update) | async-done | bytes 1572880 | tf_op jit(solution)/shard_map/psum | solution.py:54
  186.5 0.0 copy-done
  186.5 2.5 fusion.13
  189.0 0.0 copy-start.1
  189.0 1.8 copy.39
  190.8 18.0 %all-to-all-start.1 = ((bf16[128,4,1024]{2,1,0:T(4,128)(2,1)}), bf16[128,4,1024]{2,1,0:T(4,128)(2,1)}, u32[]{:S(2)}, u32[]{:S(2)}) async-start(bf16[128,4,1024]{2,1,0:T(4,128)(2,1)} %copy.39), calls=%async_computation.1 | async-start | bytes 2097152 | tf_op jit(solution)/shard_map/all_to_all | solution.py:61
  208.8 0.0 copy-done.1
  208.9 0.1 copy.32
  209.0 0.1 select_reduce_fusion
  209.1 0.1 copy.33
  209.2 55.1 %all-to-all-done.1 = bf16[128,4,1024]{2,1,0:T(4,128)(2,1)} async-done(((bf16[128,4,1024]{2,1,0:T(4,128)(2,1)}), bf16[128,4,1024]{2,1,0:T(4,128)(2,1)}, u32[]{:S(2)}, u32[]{:S(2)}) %all-to-all-start.1) | async-done | bytes 1048608 | tf_op jit(solution)/shard_map/all_to_all | solution.py:61
  264.3 2.8 %copy.53 = bf16[32,4,4,1024]{3,1,0,2:T(4,128)(2,1)} copy(bf16[32,4,4,1024]{3,2,1,0:T(4,128)(2,1)} %bitcast.17) | data formatting | bytes 2097152 | tf_op jit(solution)/shard_map/reshape | solution.py:64
  267.1 2.6 dot_general.24
  269.7 2.2 fusion.1
  (4 shorter events, 0.0 us)
Async XLA Ops:
  6.5 180.0 %copy-start = (bf16[2,768,1024]{2,1,0:T(8,128)(2,1)S(1)}, bf16[2,768,1024]{2,1,0:T(8,128)(2,1)}, u32[]{:S(2)}) copy-start(bf16[2,768,1024]{2,1,0:T(8,128)(2,1)} %param.13) | copy-start | bytes 9437188
  6.5 180.0 %all-reduce.3.cloned.1.call-start = ((), (), s32[]{:S(2)}) async-start(), calls=%async_computation.2 | async-start | bytes 3145728 | tf_op jit(solution)/shard_map/psum | solution.py:54
  6.5 4.6 %collective-permute-start = (bf16[12,4096]{1,0:T(8,128)(2,1)}, bf16[12,4096]{1,0:T(8,128)(2,1)S(1)}, u32[]{:S(2)}, u32[]{:S(2)}) collective-permute-start(bf16[12,4096]{1,0:T(8,128)(2,1)} %param.7), channel_id=1, source_target_pairs={{0,128},{128,256},{256,384},{384,512},{512,640},{640,768},{768,896... | collective-permute-start | bytes 294920 | tf_op jit(solution)/shard_map/ppermute | solution.py:11
  13.5 81.4 %copy-start.2 = (bf16[2,1024,768]{2,1,0:T(8,128)(2,1)S(1)}, bf16[2,1024,768]{2,1,0:T(8,128)(2,1)}, u32[]{:S(2)}) copy-start(bf16[2,1024,768]{2,1,0:T(8,128)(2,1)} %param.12) | copy-start | bytes 9437188
  94.9 1.9 copy-start.3
  189.0 19.9 %copy-start.1 = (f32[12,8]{0,1:T(8,128)S(1)}, f32[12,8]{0,1:T(8,128)}, u32[]{:S(2)}) copy-start(f32[12,8]{0,1:T(8,128)} %param.10) | copy-start | bytes 1156
  190.8 73.5 %all-to-all-start.1 = ((bf16[128,4,1024]{2,1,0:T(4,128)(2,1)}), bf16[128,4,1024]{2,1,0:T(4,128)(2,1)}, u32[]{:S(2)}, u32[]{:S(2)}) async-start(bf16[128,4,1024]{2,1,0:T(4,128)(2,1)} %copy.39), calls=%async_computation.1 | async-start | bytes 2097152 | tf_op jit(solution)/shard_map/all_to_all | solution.py:61
Sparse Core Ops, SparseCore 0:
  98.9 87.5 all-reduce.2

commit v2 on v1

--- a/solution.py
+++ b/solution.py
@@ -49,11 +49,20 @@
     grouped = incoming.reshape(devices, experts_here, CAP, width_part)
     gate_part = jnp.einsum("nxcd,xdf->nxcf", grouped, w_gate, preferred_element_type=jnp.float32)
     up_part = jnp.einsum("nxcd,xdf->nxcf", grouped, w_up, preferred_element_type=jnp.float32)
-    gate_full, up_full = (
-        lax.psum(gate_part.astype(jnp.bfloat16), "dp").astype(jnp.float32),
-        lax.psum(up_part.astype(jnp.bfloat16), "dp").astype(jnp.float32),
-    )
-    hidden = (jax.nn.silu(gate_full) * up_full).astype(jnp.bfloat16)
+    chunks = gate_part.shape[0] // dp_groups
+    parts = jnp.stack(
+        [
+            gate_part.reshape(dp_groups, chunks, experts_here, CAP, -1),
+            up_part.reshape(dp_groups, chunks, experts_here, CAP, -1),
+        ],
+        axis=1,
+    ).astype(jnp.bfloat16)
+    parts = lax.all_to_all(parts, "dp", split_axis=0, concat_axis=0, tiled=False)
+    summed = jnp.sum(parts.astype(jnp.float32), axis=0)
+    gate_full, up_full = summed[0], summed[1]
+    hidden_chunk = (jax.nn.silu(gate_full) * up_full).astype(jnp.bfloat16)
+    hidden = lax.all_gather(hidden_chunk, "dp", axis=0, tiled=True)
+    hidden = hidden.reshape(devices, experts_here, CAP, -1)
     expert_out = jnp.einsum(
         "nxcf,xfd->nxcd", hidden, w_down, preferred_element_type=jnp.float32
     ).astype(jnp.bfloat16)

time: 279 us -> 225 us (0.81)
  waiting for transfers between devices: 146 us -> 55.4 us
  blocking collectives: 81.1 us -> 136 us
  between operations: 13.5 us -> 0.17 us
  matrix products: 8.91 us -> 5.65 us
  starting transfers between devices: 18 us -> 14.9 us
    psum x1 -> x0, waiting for transfers between devices: 87.8 us -> none  [per_device(): lax.psum(up_part.astype(jnp.bfloat16), 'dp').astype(jnp.float32)]
    all_to_all x0 -> x1, blocking collectives: none -> 35.1 us  [per_device(): lax.all_to_all(parts, 'dp', split_axis=0, concat_axis=0, tiled=False)]
    all_gather x0 -> x1, blocking collectives: none -> 19.8 us  [per_device(): hidden = lax.all_gather(hidden_chunk, 'dp', axis=0, tiled=True)]
    all_to_all x1, starting transfers between devices: 18 us -> 14.9 us  [per_device(): lax.all_to_all(returning, ('expert', 'dp'), split_axis=0, concat_axis=0,...]
  transfers between devices with their start and end apart: 3 -> 2, of which waited for: 3 -> 2; matrix products, arithmetic and copies ran while one was open for 1% -> 1% of each run, Pallas kernels for 0% -> 0%
where the time goes in v2:
time: 225 us
  blocking collectives  136 us (60%)
  waiting for transfers between devices  55.4 us (25%)
  starting transfers between devices  14.9 us (7%)
  local copies, waits for them, and re-layouts  10.7 us (5%)
  matrix products  5.65 us (3%)
    all_to_all x1, blocking collectives, per_device(): lax.all_to_all(outgoing, ('expert', 'dp'), split_axis=0, concat_axis=0, t...  80.9 us
    all_to_all x1, waiting for transfers between devices, per_device(): lax.all_to_all(returning, ('expert', 'dp'), split_axis=0, concat_axis=0,...  52.7 us
    all_to_all x1, blocking collectives, per_device(): lax.all_to_all(parts, 'dp', split_axis=0, concat_axis=0, tiled=False)  35.1 us
    all_gather x1, blocking collectives, per_device(): hidden = lax.all_gather(hidden_chunk, 'dp', axis=0, tiled=True)  19.8 us
    all_to_all x1, starting transfers between devices, per_device(): lax.all_to_all(returning, ('expert', 'dp'), split_axis=0, concat_axis=0,...  14.9 us
  transfers between devices with their start and end apart: 2, of which 2 were waited for; matrix products, arithmetic and copies ran while one was open for 1% of the time, Pallas kernels for 0%

profile of v2, /device:TPU:26, one launch (start us, length us, event | category | flops | bytes accessed | tf_op | source)
XLA Modules:
  0.0 224.8 jit_solution(2752607008393214345)
XLA Ops:
  0.0 0.0 copy-start
  0.0 0.0 collective-permute-start
  0.0 0.9 copy.32
  0.9 0.1 eq.29
  1.0 0.1 fusion.25
  1.1 0.1 reduce_window_sum.11
  1.2 0.2 select_reduce_fusion.1
  1.4 0.1 reduce_sum.48
  1.5 0.1 fusion.24
  1.6 0.1 copy.36
  1.8 0.1 copy.38
  1.9 2.7 %collective-permute-done = bf16[12,4096]{1,0:T(8,128)(2,1)S(1)} collective-permute-done((bf16[12,4096]{1,0:T(8,128)(2,1)}, bf16[12,4096]{1,0:T(8,128)(2,1)S(1)}, u32[]{:S(2)}, u32[]{:S(2)}) %collective-permute-start) | collective-permute-done | bytes 98336 | tf_op jit(solution)/shard_map/ppermute | solution.py:11
  4.6 0.1 fusion.20
  4.8 0.8 fusion.22
  5.6 0.1 reshape.60
  5.7 0.5 fusion.17
  6.2 0.0 copy-start.2
  6.2 0.8 copy.39
  7.0 80.9 %all_to_all.15 = bf16[128,4,1024]{2,1,0:T(4,128)(2,1)S(1)} all-to-all(bf16[128,4,1024]{2,1,0:T(4,128)(2,1)S(1)} %bitcast.67), channel_id=1, replica_groups=mesh['section'=8,'expert'=32,'dp'=4] {'expert','dp'}, dimensions={0} | all-to-all | bytes 2097152 | tf_op jit(solution)/shard_map/all_to_all | solution.py:46
  87.9 0.0 copy-start.3
  87.9 0.3 copy.40
  88.3 0.0 copy-done.2
  88.3 1.0 fusion.11
  89.3 0.6 copy-done.3
  89.8 1.0 fusion.14
  90.8 0.1 pad_maximum_fusion
  91.0 0.1 copy.52
  91.1 35.1 %all_to_all.16 = bf16[4,2,32,2,2,768]{5,2,4,3,1,0:T(8,128)(2,1)S(1)} all-to-all(bf16[4,2,32,2,2,768]{5,2,4,3,1,0:T(8,128)(2,1)S(1)} %copy.52), channel_id=1, replica_groups=mesh['section'=8,'expert'=32,'dp'=4] {'dp'}, dimensions={0} | all-to-all | bytes 3145728 | tf_op jit(solution)/shard_map/all_to_all | solution.py:60
  126.2 0.2 convert_reduce_fusion
  126.5 0.1 fusion.19
  126.6 19.8 %all_gather.3 = bf16[128,2,2,768]{3,0,2,1:T(8,128)(2,1)S(1)} all-gather(bf16[32,2,2,768]{3,0,2,1:T(8,128)(2,1)S(1)} %fusion.19), channel_id=1, replica_groups=mesh['section'=8,'expert'=32,'dp'=4] {'dp'}, dimensions={0}, use_global_device_ids=true | all-gather | bytes 983040 | tf_op jit(solution)/shard_map/all_gather | solution.py:64
  146.4 0.0 copy-done
  146.4 1.0 fusion.8
  147.4 0.0 copy-start.1
  147.4 1.8 copy.43
  149.3 14.9 %all-to-all-start.2 = ((bf16[128,4,1024]{2,1,0:T(4,128)(2,1)}), bf16[128,4,1024]{2,1,0:T(4,128)(2,1)}, u32[]{:S(2)}, u32[]{:S(2)}) async-start(bf16[128,4,1024]{2,1,0:T(4,128)(2,1)} %copy.43), calls=%async_computation.2 | async-start | bytes 2097152 | tf_op jit(solution)/shard_map/all_to_all | solution.py:70
  164.1 0.0 copy-done.1
  164.2 0.1 copy.34
  164.3 0.1 select_reduce_fusion
  164.4 0.1 copy.35
  164.5 52.7 %all-to-all-done.2 = bf16[128,4,1024]{2,1,0:T(4,128)(2,1)} async-done(((bf16[128,4,1024]{2,1,0:T(4,128)(2,1)}), bf16[128,4,1024]{2,1,0:T(4,128)(2,1)}, u32[]{:S(2)}, u32[]{:S(2)}) %all-to-all-start.2) | async-done | bytes 1048608 | tf_op jit(solution)/shard_map/all_to_all | solution.py:70
  217.2 2.8 %copy.58 = bf16[32,4,4,1024]{3,1,0,2:T(4,128)(2,1)} copy(bf16[32,4,4,1024]{3,2,1,0:T(4,128)(2,1)} %bitcast.21) | data formatting | bytes 2097152 | tf_op jit(solution)/shard_map/reshape | solution.py:73
  220.0 2.6 %dot_general.24 = bf16[4096,32,4]{0,1,2:T(8,128)(2,1)} reshape(bf16[4,1024,32,4]{1,0,2,3:T(4,128)(2,1)} %bitcast.68) | data formatting | bytes 2097152 | tf_op jit(solution)/shard_map/tes,epsw->tpw/dot_general | solution.py:78
  222.6 2.2 fusion.1
  (4 shorter events, 0.0 us)
Async XLA Ops:
  0.0 146.4 %copy-start = (bf16[2,768,1024]{2,1,0:T(8,128)(2,1)S(1)}, bf16[2,768,1024]{2,1,0:T(8,128)(2,1)}, u32[]{:S(2)}) copy-start(bf16[2,768,1024]{2,1,0:T(8,128)(2,1)} %param.13) | copy-start | bytes 9437188
  0.0 4.6 %collective-permute-start = (bf16[12,4096]{1,0:T(8,128)(2,1)}, bf16[12,4096]{1,0:T(8,128)(2,1)S(1)}, u32[]{:S(2)}, u32[]{:S(2)}) collective-permute-start(bf16[12,4096]{1,0:T(8,128)(2,1)} %param.7), channel_id=1, source_target_pairs={{0,128},{128,256},{256,384},{384,512},{512,640},{640,768},{768,896... | collective-permute-start | bytes 294920 | tf_op jit(solution)/shard_map/ppermute | solution.py:11
  6.2 82.1 %copy-start.2 = (bf16[2,1024,768]{2,1,0:T(8,128)(2,1)S(1)}, bf16[2,1024,768]{2,1,0:T(8,128)(2,1)}, u32[]{:S(2)}) copy-start(bf16[2,1024,768]{2,1,0:T(8,128)(2,1)} %param.11) | copy-start | bytes 9437188
  87.9 1.9 copy-start.3
  147.4 16.7 %copy-start.1 = (f32[12,8]{0,1:T(8,128)S(1)}, f32[12,8]{0,1:T(8,128)}, u32[]{:S(2)}) copy-start(f32[12,8]{0,1:T(8,128)} %param.10) | copy-start | bytes 1156
  149.3 67.9 %all-to-all-start.2 = ((bf16[128,4,1024]{2,1,0:T(4,128)(2,1)}), bf16[128,4,1024]{2,1,0:T(4,128)(2,1)}, u32[]{:S(2)}, u32[]{:S(2)}) async-start(bf16[128,4,1024]{2,1,0:T(4,128)(2,1)} %copy.43), calls=%async_computation.2 | async-start | bytes 2097152 | tf_op jit(solution)/shard_map/all_to_all | solution.py:70

commit v3 on v1

--- a/solution.py
+++ b/solution.py
@@ -35,38 +35,49 @@
         tokens_here, top_k, all_slots
     )
     occupied = jnp.any(placed, axis=1).astype(jnp.bfloat16).reshape(
-        tokens_here, expert_groups, slot_rows
+        tokens_here, expert_groups, experts_here, CAP
     )
-    normed_parts = normed.reshape(tokens_here, dp_groups, width_part)
-    send_rows = jnp.einsum(
-        "tes,tpw->epsw", occupied, normed_parts, preferred_element_type=jnp.float32
-    ).astype(jnp.bfloat16)
-    devices = expert_groups * dp_groups
-    outgoing = send_rows.reshape(devices, slot_rows, width_part)
-    incoming = lax.all_to_all(
-        outgoing, ("expert", "dp"), split_axis=0, concat_axis=0, tiled=True
-    )
-    grouped = incoming.reshape(devices, experts_here, CAP, width_part)
-    gate_part = jnp.einsum("nxcd,xdf->nxcf", grouped, w_gate, preferred_element_type=jnp.float32)
-    up_part = jnp.einsum("nxcd,xdf->nxcf", grouped, w_up, preferred_element_type=jnp.float32)
-    gate_full, up_full = (
-        lax.psum(gate_part.astype(jnp.bfloat16), "dp").astype(jnp.float32),
-        lax.psum(up_part.astype(jnp.bfloat16), "dp").astype(jnp.float32),
-    )
-    hidden = (jax.nn.silu(gate_full) * up_full).astype(jnp.bfloat16)
-    expert_out = jnp.einsum(
-        "nxcf,xfd->nxcd", hidden, w_down, preferred_element_type=jnp.float32
-    ).astype(jnp.bfloat16)
-    returning = expert_out.reshape(devices, slot_rows, width_part)
-    returned = lax.all_to_all(
-        returning, ("expert", "dp"), split_axis=0, concat_axis=0, tiled=True
-    )
-    back = returned.reshape(expert_groups, dp_groups, slot_rows, width_part)
     weights = (gate_scores / jnp.sum(gate_scores, axis=-1, keepdims=True)).astype(jnp.bfloat16)
     combine = jnp.sum(
         jnp.where(placed, weights[:, :, None].astype(jnp.float32), 0.0), axis=1
-    ).astype(jnp.bfloat16).reshape(tokens_here, expert_groups, slot_rows)
-    mixed = jnp.einsum("tes,epsw->tpw", combine, back, preferred_element_type=jnp.float32)
+    ).astype(jnp.bfloat16).reshape(tokens_here, expert_groups, experts_here, CAP)
+    normed_parts = normed.reshape(tokens_here, dp_groups, width_part)
+    devices = expert_groups * dp_groups
+    chunks = devices // dp_groups
+    send_rows = jnp.einsum(
+        "texc,tpw->xepcw", occupied, normed_parts, preferred_element_type=jnp.float32
+    ).astype(jnp.bfloat16)
+    mixed = jnp.zeros((tokens_here, dp_groups, width_part), jnp.float32)
+    for x in range(experts_here):
+        outgoing = send_rows[x].reshape(devices, CAP, width_part)
+        grouped = lax.all_to_all(
+            outgoing, ("expert", "dp"), split_axis=0, concat_axis=0, tiled=True
+        )
+        gate_part = jnp.einsum(
+            "ncd,df->ncf", grouped, w_gate[x], preferred_element_type=jnp.float32
+        )
+        up_part = jnp.einsum("ncd,df->ncf", grouped, w_up[x], preferred_element_type=jnp.float32)
+        parts = jnp.stack(
+            [
+                gate_part.reshape(dp_groups, chunks, CAP, -1),
+                up_part.reshape(dp_groups, chunks, CAP, -1),
+            ],
+            axis=1,
+        ).astype(jnp.bfloat16)
+        parts = lax.all_to_all(parts, "dp", split_axis=0, concat_axis=0, tiled=False)
+        summed = jnp.sum(parts.astype(jnp.float32), axis=0)
+        hidden_chunk = (jax.nn.silu(summed[0]) * summed[1]).astype(jnp.bfloat16)
+        hidden = lax.all_gather(hidden_chunk, "dp", axis=0, tiled=True)
+        expert_out = jnp.einsum(
+            "ncf,fd->ncd", hidden, w_down[x], preferred_element_type=jnp.float32
+        ).astype(jnp.bfloat16)
+        returned = lax.all_to_all(
+            expert_out, ("expert", "dp"), split_axis=0, concat_axis=0, tiled=True
+        )
+        back = returned.reshape(expert_groups, dp_groups, CAP, width_part)
+        mixed = mixed + jnp.einsum(
+            "tec,epcw->tpw", combine[:, :, x], back, preferred_element_type=jnp.float32
+        )
     mixed_out = arrived_f + mixed.reshape(tokens_here, dp_groups * width_part)
     return mixed_out.astype(jnp.bfloat16)
 

time: 279 us -> 251 us (0.90)
  the two profiles are of different devices: /device:TPU:26 before, /device:TPU:10 now
where the time goes in v3:
time: 251 us
  waiting for transfers between devices  122 us (49%)
  starting transfers between devices  58.9 us (23%)
  blocking collectives  46 us (18%)
  matrix products  10.8 us (4%)
  local copies, waits for them, and re-layouts  9.79 us (4%)
  other arithmetic  2.81 us (1%)
    all_to_all x2, waiting for transfers between devices, per_device(): lax.all_to_all(outgoing, ('expert', 'dp'), split_axis=0, concat_axis=0, t...  64.1 us
    all_gather x2, blocking collectives, per_device(): hidden = lax.all_gather(hidden_chunk, 'dp', axis=0, tiled=True)  46 us
    all_to_all x2, waiting for transfers between devices, per_device(): lax.all_to_all(expert_out, ('expert', 'dp'), split_axis=0, concat_axis=0,...  41.2 us
    all_to_all x2, starting transfers between devices, per_device(): lax.all_to_all(outgoing, ('expert', 'dp'), split_axis=0, concat_axis=0, t...  31.8 us
    all_to_all x2, starting transfers between devices, per_device(): lax.all_to_all(expert_out, ('expert', 'dp'), split_axis=0, concat_axis=0,...  20.1 us
    all_to_all x2, waiting for transfers between devices, per_device(): lax.all_to_all(parts, 'dp', split_axis=0, concat_axis=0, tiled=False)  13.9 us
    all_to_all x2, starting transfers between devices, per_device(): lax.all_to_all(parts, 'dp', split_axis=0, concat_axis=0, tiled=False)  6.99 us
  transfers between devices with their start and end apart: 7, of which 6 were waited for; matrix products, arithmetic and copies ran while one was open for 8% of the time, Pallas kernels for 0%

profile of v3, /device:TPU:10, one launch (start us, length us, event | category | flops | bytes accessed | tf_op | source)
XLA Modules:
  0.0 250.5 jit_solution(6292317979938998731)
XLA Ops:
  0.0 0.0 collective-permute-start
  0.0 0.8 copy.74
  0.8 0.1 eq.29
  0.9 0.1 fusion.66
  0.9 0.1 reduce_window_sum.11
  1.1 0.2 select_reduce_fusion.1
  1.3 0.1 reduce_sum.57
  1.4 0.1 fusion.65
  1.5 0.1 copy.79
  1.7 0.1 copy.81
  1.8 2.8 %collective-permute-done = bf16[12,4096]{1,0:T(8,128)(2,1)S(1)} collective-permute-done((bf16[12,4096]{1,0:T(8,128)(2,1)}, bf16[12,4096]{1,0:T(8,128)(2,1)S(1)}, u32[]{:S(2)}, u32[]{:S(2)}) %collective-permute-start) | collective-permute-done | bytes 98336 | tf_op jit(solution)/shard_map/ppermute | solution.py:11
  4.6 0.1 fusion.56
  4.8 0.8 fusion.58
  5.6 0.1 reshape.73
  5.7 0.5 fusion.18
  6.2 0.1 fusion.71
  6.3 1.3 copy.82
  7.6 25.8 %all-to-all-start = ((bf16[128,2,1024]{2,1,0:T(2,128)(2,1)}), bf16[128,2,1024]{2,1,0:T(2,128)(2,1)S(1)}, u32[]{:S(2)}, u32[]{:S(2)}) async-start(bf16[128,2,1024]{2,1,0:T(2,128)(2,1)} %bitcast.6), calls=%async_computation | async-start | bytes 1048576 | tf_op jit(solution)/shard_map/all_to_all | solution.py:53
  33.4 1.3 copy.90
  34.7 33.2 %all-to-all-done = bf16[128,2,1024]{2,1,0:T(2,128)(2,1)S(1)} async-done(((bf16[128,2,1024]{2,1,0:T(2,128)(2,1)}), bf16[128,2,1024]{2,1,0:T(2,128)(2,1)S(1)}, u32[]{:S(2)}, u32[]{:S(2)}) %all-to-all-start) | async-done | bytes 524320 | tf_op jit(solution)/shard_map/all_to_all | solution.py:53
  67.9 6.0 %all-to-all-start.3 = ((bf16[128,2,1024]{2,1,0:T(2,128)(2,1)}), bf16[128,2,1024]{2,1,0:T(2,128)(2,1)S(1)}, u32[]{:S(2)}, u32[]{:S(2)}) async-start(bf16[128,2,1024]{2,1,0:T(2,128)(2,1)} %bitcast.25), calls=%async_computation.3 | async-start | bytes 1048576 | tf_op jit(solution)/shard_map/all_to_all | solution.py:53
  73.9 0.0 copy-start.1
  73.9 0.1 copy.83
  74.1 2.1 fusion.43
  76.2 0.1 copy-done.1
  76.3 0.6 fusion.46
  76.9 0.1 pad_maximum_fusion
  77.0 0.9 copy.86
  77.9 30.9 %all-to-all-done.3 = bf16[128,2,1024]{2,1,0:T(2,128)(2,1)S(1)} async-done(((bf16[128,2,1024]{2,1,0:T(2,128)(2,1)}), bf16[128,2,1024]{2,1,0:T(2,128)(2,1)S(1)}, u32[]{:S(2)}, u32[]{:S(2)}) %all-to-all-start.3) | async-done | bytes 524320 | tf_op jit(solution)/shard_map/all_to_all | solution.py:53
  108.8 3.5 %all-to-all-start.1 = ((bf16[4,2,32,2,768]{4,2,3,1,0:T(8,128)(2,1)}), bf16[4,2,32,2,768]{4,2,3,1,0:T(8,128)(2,1)S(1)}, u32[]{:S(2)}, u32[]{:S(2)}) async-start(bf16[4,2,32,2,768]{4,2,3,1,0:T(8,128)(2,1)} %copy.86), calls=%async_computation.1 | async-start | bytes 1572864 | tf_op jit(solution)/shard_map/all_to_all | solution.py:67
  112.3 0.0 copy-start.2
  112.3 0.1 copy.91
  112.4 2.1 fusion.37
  114.6 0.1 copy-done.2
  114.7 0.6 fusion.40
  115.2 0.1 pad_maximum_fusion.1
  115.3 1.0 copy.94
  116.3 13.9 %all-to-all-done.1 = bf16[4,2,32,2,768]{4,2,3,1,0:T(8,128)(2,1)S(1)} async-done(((bf16[4,2,32,2,768]{4,2,3,1,0:T(8,128)(2,1)}), bf16[4,2,32,2,768]{4,2,3,1,0:T(8,128)(2,1)S(1)}, u32[]{:S(2)}, u32[]{:S(2)}) %all-to-all-start.1) | async-done | bytes 786464 | tf_op jit(solution)/shard_map/all_to_all | solution.py:67
  130.2 3.5 %all-to-all-start.4 = ((bf16[4,2,32,2,768]{4,2,3,1,0:T(8,128)(2,1)}), bf16[4,2,32,2,768]{4,2,3,1,0:T(8,128)(2,1)S(1)}, u32[]{:S(2)}, u32[]{:S(2)}) async-start(bf16[4,2,32,2,768]{4,2,3,1,0:T(8,128)(2,1)} %copy.94), calls=%async_computation.4 | async-start | bytes 1572864 | tf_op jit(solution)/shard_map/all_to_all | solution.py:67
  133.7 0.1 convert_reduce_fusion.1
  133.8 0.1 fusion.63
  133.9 27.9 %all_gather.6 = bf16[128,2,768]{2,0,1:T(8,128)(2,1)S(1)} all-gather(bf16[32,2,768]{2,0,1:T(8,128)(2,1)S(1)} %fusion.63), channel_id=1, replica_groups=mesh['section'=8,'expert'=32,'dp'=4] {'dp'}, dimensions={0}, use_global_device_ids=true | all-gather | bytes 491520 | tf_op jit(solution)/shard_map/all_gather | solution.py:70
  161.8 2.0 fusion.19
  163.8 1.3 copy.87
  165.1 12.8 %all-to-all-start.2 = ((bf16[128,2,1024]{2,1,0:T(2,128)(2,1)}), bf16[128,2,1024]{2,1,0:T(2,128)(2,1)S(1)}, u32[]{:S(2)}, u32[]{:S(2)}) async-start(bf16[128,2,1024]{2,1,0:T(2,128)(2,1)} %copy.87), calls=%async_computation.2 | async-start | bytes 1048576 | tf_op jit(solution)/shard_map/all_to_all | solution.py:74
  178.0 0.1 convert_reduce_fusion
  178.1 0.0 copy-start
  178.1 0.1 fusion.61
  178.2 18.1 %all_gather.7 = bf16[128,2,768]{2,0,1:T(8,128)(2,1)S(1)} all-gather(bf16[32,2,768]{2,0,1:T(8,128)(2,1)S(1)} %fusion.61), channel_id=1, replica_groups=mesh['section'=8,'expert'=32,'dp'=4] {'dp'}, dimensions={0}, use_global_device_ids=true | all-gather | bytes 491520 | tf_op jit(solution)/shard_map/all_gather | solution.py:70
  196.2 2.0 fusion.22
  198.3 1.4 copy.95
  199.6 10.6 %all-to-all-done.2 = bf16[128,2,1024]{2,1,0:T(2,128)(2,1)S(1)} async-done(((bf16[128,2,1024]{2,1,0:T(2,128)(2,1)}), bf16[128,2,1024]{2,1,0:T(2,128)(2,1)S(1)}, u32[]{:S(2)}, u32[]{:S(2)}) %all-to-all-start.2) | async-done | bytes 524320 | tf_op jit(solution)/shard_map/all_to_all | solution.py:74
  210.2 7.2 %all-to-all-start.5 = ((bf16[128,2,1024]{2,1,0:T(2,128)(2,1)}), bf16[128,2,1024]{2,1,0:T(2,128)(2,1)S(1)}, u32[]{:S(2)}, u32[]{:S(2)}) async-start(bf16[128,2,1024]{2,1,0:T(2,128)(2,1)} %copy.95), calls=%async_computation.5 | async-start | bytes 1048576 | tf_op jit(solution)/shard_map/all_to_all | solution.py:74
  217.5 0.1 copy.76
  217.6 0.1 select_reduce_fusion
  217.7 0.1 copy.77
  217.9 0.1 copy.107
  218.0 0.1 copy.108
  218.0 0.4 convolution_bitcast_fusion.1
  218.5 30.6 %all-to-all-done.5 = bf16[128,2,1024]{2,1,0:T(2,128)(2,1)S(1)} async-done(((bf16[128,2,1024]{2,1,0:T(2,128)(2,1)}), bf16[128,2,1024]{2,1,0:T(2,128)(2,1)S(1)}, u32[]{:S(2)}, u32[]{:S(2)}) %all-to-all-start.5) | async-done | bytes 524320 | tf_op jit(solution)/shard_map/all_to_all | solution.py:74
  249.1 0.4 fusion.49
  249.5 0.1 copy.97
  249.7 0.2 copy.109
  249.8 0.7 fusion.59
  (9 shorter events, 0.2 us)
Async XLA Ops:
  0.0 4.6 %collective-permute-start = (bf16[12,4096]{1,0:T(8,128)(2,1)}, bf16[12,4096]{1,0:T(8,128)(2,1)S(1)}, u32[]{:S(2)}, u32[]{:S(2)}) collective-permute-start(bf16[12,4096]{1,0:T(8,128)(2,1)} %param.7), channel_id=1, source_target_pairs={{0,128},{128,256},{256,384},{384,512},{512,640},{640,768},{768,896... | collective-permute-start | bytes 294920 | tf_op jit(solution)/shard_map/ppermute | solution.py:11
  7.6 60.3 %all-to-all-start = ((bf16[128,2,1024]{2,1,0:T(2,128)(2,1)}), bf16[128,2,1024]{2,1,0:T(2,128)(2,1)S(1)}, u32[]{:S(2)}, u32[]{:S(2)}) async-start(bf16[128,2,1024]{2,1,0:T(2,128)(2,1)} %bitcast.6), calls=%async_computation | async-start | bytes 1048576 | tf_op jit(solution)/shard_map/all_to_all | solution.py:53
  67.9 40.9 %all-to-all-start.3 = ((bf16[128,2,1024]{2,1,0:T(2,128)(2,1)}), bf16[128,2,1024]{2,1,0:T(2,128)(2,1)S(1)}, u32[]{:S(2)}, u32[]{:S(2)}) async-start(bf16[128,2,1024]{2,1,0:T(2,128)(2,1)} %bitcast.25), calls=%async_computation.3 | async-start | bytes 1048576 | tf_op jit(solution)/shard_map/all_to_all | solution.py:53
  73.9 2.4 copy-start.1
  108.8 21.4 %all-to-all-start.1 = ((bf16[4,2,32,2,768]{4,2,3,1,0:T(8,128)(2,1)}), bf16[4,2,32,2,768]{4,2,3,1,0:T(8,128)(2,1)S(1)}, u32[]{:S(2)}, u32[]{:S(2)}) async-start(bf16[4,2,32,2,768]{4,2,3,1,0:T(8,128)(2,1)} %copy.86), calls=%async_computation.1 | async-start | bytes 1572864 | tf_op jit(solution)/shard_map/all_to_all | solution.py:67
  112.3 2.4 copy-start.2
  130.2 34.9 %all-to-all-start.4 = ((bf16[4,2,32,2,768]{4,2,3,1,0:T(8,128)(2,1)}), bf16[4,2,32,2,768]{4,2,3,1,0:T(8,128)(2,1)S(1)}, u32[]{:S(2)}, u32[]{:S(2)}) async-start(bf16[4,2,32,2,768]{4,2,3,1,0:T(8,128)(2,1)} %copy.94), calls=%async_computation.4 | async-start | bytes 1572864 | tf_op jit(solution)/shard_map/all_to_all | solution.py:67
  165.1 45.1 %all-to-all-start.2 = ((bf16[128,2,1024]{2,1,0:T(2,128)(2,1)}), bf16[128,2,1024]{2,1,0:T(2,128)(2,1)S(1)}, u32[]{:S(2)}, u32[]{:S(2)}) async-start(bf16[128,2,1024]{2,1,0:T(2,128)(2,1)} %copy.87), calls=%async_computation.2 | async-start | bytes 1048576 | tf_op jit(solution)/shard_map/all_to_all | solution.py:74
  178.1 39.4 %copy-start = (f32[12,8]{0,1:T(8,128)S(1)}, f32[12,8]{0,1:T(8,128)}, u32[]{:S(2)}) copy-start(f32[12,8]{0,1:T(8,128)} %param.10) | copy-start | bytes 1156
  210.2 38.9 %all-to-all-start.5 = ((bf16[128,2,1024]{2,1,0:T(2,128)(2,1)}), bf16[128,2,1024]{2,1,0:T(2,128)(2,1)S(1)}, u32[]{:S(2)}, u32[]{:S(2)}) async-start(bf16[128,2,1024]{2,1,0:T(2,128)(2,1)} %copy.95), calls=%async_computation.5 | async-start | bytes 1048576 | tf_op jit(solution)/shard_map/all_to_all | solution.py:74

commit v4 on v2

--- a/solution.py
+++ b/solution.py
@@ -37,16 +37,22 @@
     occupied = jnp.any(placed, axis=1).astype(jnp.bfloat16).reshape(
         tokens_here, expert_groups, slot_rows
     )
+    devices = expert_groups * dp_groups
     normed_parts = normed.reshape(tokens_here, dp_groups, width_part)
-    send_rows = jnp.einsum(
-        "tes,tpw->epsw", occupied, normed_parts, preferred_element_type=jnp.float32
+    gathered = lax.all_to_all(normed_parts, "dp", split_axis=1, concat_axis=0, tiled=True)
+    gathered = lax.all_gather(gathered, "expert", axis=0, tiled=True)
+    tokens_all = gathered.reshape(devices, tokens_here, width_part)
+    ids_all = lax.all_gather(expert_ids, ("expert", "dp"), axis=0, tiled=True)
+    ids_all = ids_all.reshape(devices, tokens_here, top_k)
+    mine = lax.axis_index("expert") * experts_here + jnp.arange(experts_here, dtype=jnp.int32)
+    hits = jnp.any(ids_all[:, :, :, None] == mine[None, None, None, :], axis=2).astype(jnp.int32)
+    before = jnp.cumsum(hits, axis=1) - hits
+    pick = (hits[:, :, :, None] == 1) & (
+        before[:, :, :, None] == jnp.arange(CAP, dtype=jnp.int32)[None, None, None, :]
+    )
+    grouped = jnp.einsum(
+        "ntxc,ntw->nxcw", pick.astype(jnp.bfloat16), tokens_all, preferred_element_type=jnp.float32
     ).astype(jnp.bfloat16)
-    devices = expert_groups * dp_groups
-    outgoing = send_rows.reshape(devices, slot_rows, width_part)
-    incoming = lax.all_to_all(
-        outgoing, ("expert", "dp"), split_axis=0, concat_axis=0, tiled=True
-    )
-    grouped = incoming.reshape(devices, experts_here, CAP, width_part)
     gate_part = jnp.einsum("nxcd,xdf->nxcf", grouped, w_gate, preferred_element_type=jnp.float32)
     up_part = jnp.einsum("nxcd,xdf->nxcf", grouped, w_up, preferred_element_type=jnp.float32)
     chunks = gate_part.shape[0] // dp_groups

time: 225 us -> 468 us (2.08)
  the two profiles are of different devices: /device:TPU:26 before, /device:TPU:28 now
where the time goes in v4:
time: 468 us; the launch traced here: 467 us
  blocking collectives  374 us (80%)
  waiting for transfers between devices  38.4 us (8%)
  local copies, waits for them, and re-layouts  17.1 us (4%)
  between operations  13.6 us (3%)
  starting transfers between devices  13.2 us (3%)
  matrix products  8.89 us (2%)
    all_gather x1, blocking collectives, per_device(): ids_all = lax.all_gather(expert_ids, ('expert', 'dp'), axis=0, tiled=True)  311 us
    all_to_all x1, waiting for transfers between devices, per_device(): lax.all_to_all(returning, ('expert', 'dp'), split_axis=0, concat_axis=0,...  33.8 us
    all_to_all x1, blocking collectives, per_device(): lax.all_to_all(parts, 'dp', split_axis=0, concat_axis=0, tiled=False)  33.2 us
    all_gather x1, blocking collectives, per_device(): hidden = lax.all_gather(hidden_chunk, 'dp', axis=0, tiled=True)  16.4 us
    all_to_all x1, starting transfers between devices, per_device(): lax.all_to_all(returning, ('expert', 'dp'), split_axis=0, concat_axis=0,...  13.2 us
    all_to_all x1, blocking collectives, per_device(): lax.all_to_all(normed_parts, 'dp', split_axis=1, concat_axis=0, tiled=True)  12.8 us
  transfers between devices with their start and end apart: 3, of which 2 were waited for; matrix products, arithmetic and copies ran while one was open for 1% of the time, Pallas kernels for 0%

profile of v4, /device:TPU:28, one launch (start us, length us, event | category | flops | bytes accessed | tf_op | source)
XLA Modules:
  0.0 467.2 jit_solution(13472192990200221361)
XLA Ops:
  6.5 0.0 copy-start
  6.5 0.0 all-gather.3.cloned.1.call-start
  6.5 0.0 collective-permute-start
  6.5 4.6 collective-permute-done
  11.1 0.1 fusion.28
  11.3 0.8 fusion.30
  12.1 0.1 reshape.75
  12.2 12.8 %all_to_all.28 = bf16[12,4,1024]{2,0,1:T(8,128)(2,1)S(1)} all-to-all(bf16[12,4,1024]{2,0,1:T(8,128)(2,1)S(1)} %copy.42), channel_id=1, replica_groups=mesh['section'=8,'expert'=32,'dp'=4] {'dp'}, dimensions={1} | all-to-all | bytes 196608 | tf_op jit(solution)/shard_map/all_to_all | solution.py:42
  25.0 0.7 all_to_all.22
  25.7 0.0 all-gather.3.cloned.1.call-update
  25.7 311.4 %all-gather = s32[128,12,8]{1,2,0:T(8,128)} all-gather(s32[1,12,8]{1,2,0:T(8,128)} %bitcast.74), channel_id=1, replica_groups=mesh['section'=8,'expert'=32,'dp'=4] {'expert','dp'}, dimensions={0}, use_global_device_ids=true | all-gather | bytes 49536 | tf_op jit(solution)/shard_map/all_gather | solution.py:45
  337.2 1.2 copy.39
  338.4 0.1 compare_reduce_fusion
  338.5 0.1 copy.41
  338.7 0.2 copy.40
  338.9 0.0 all-gather.3.cloned.1.call-done
  338.9 6.1 %reshape.82 = bf16[128,12,1024,1]{2,1,0,3:T(8,128)(2,1)} reshape(bf16[1536,1,1024]{2,0,1:T(8,128)(2,1)} %all-gather.3.cloned.1.call-done) | data formatting | bytes 6291456 | tf_op jit(solution)/shard_map/reshape | solution.py:44
  345.0 0.0 copy-start.3
  345.0 3.6 fusion.10
  348.6 0.0 copy-done.3
  348.6 0.0 copy-start.4
  348.6 1.0 fusion.19
  349.7 0.8 copy-done.4
  350.5 1.1 fusion.16
  351.6 0.1 pad_maximum_fusion
  351.7 0.1 copy.54
  351.9 33.2 %all_to_all.29 = bf16[4,2,32,2,2,768]{5,2,4,3,1,0:T(8,128)(2,1)S(1)} all-to-all(bf16[4,2,32,2,2,768]{5,2,4,3,1,0:T(8,128)(2,1)S(1)} %copy.54), channel_id=1, replica_groups=mesh['section'=8,'expert'=32,'dp'=4] {'dp'}, dimensions={0} | all-to-all | bytes 3145728 | tf_op jit(solution)/shard_map/all_to_all | solution.py:66
  385.1 0.2 convert_reduce_fusion
  385.3 0.1 fusion.27
  385.4 16.4 %all_gather.11 = bf16[128,2,2,768]{3,0,2,1:T(8,128)(2,1)S(1)} all-gather(bf16[32,2,2,768]{3,0,2,1:T(8,128)(2,1)S(1)} %fusion.27), channel_id=1, replica_groups=mesh['section'=8,'expert'=32,'dp'=4] {'dp'}, dimensions={0}, use_global_device_ids=true | all-gather | bytes 983040 | tf_op jit(solution)/shard_map/all_gather | solution.py:70
  401.9 0.0 copy-done
  401.9 1.0 fusion.13
  402.9 0.0 copy-start.1
  402.9 0.0 copy-start.2
  402.9 1.8 copy.47
  404.7 13.2 %all-to-all-start.2 = ((bf16[128,4,1024]{2,1,0:T(4,128)(2,1)}), bf16[128,4,1024]{2,1,0:T(4,128)(2,1)}, u32[]{:S(2)}, u32[]{:S(2)}) async-start(bf16[128,4,1024]{2,1,0:T(4,128)(2,1)} %copy.47), calls=%async_computation.2 | async-start | bytes 2097152 | tf_op jit(solution)/shard_map/all_to_all | solution.py:76
  417.9 0.0 copy-done.1
  417.9 0.1 copy.35
  418.0 0.1 eq.68
  418.1 0.1 fusion.34
  418.2 0.1 reduce_window_sum.22
  418.3 0.2 select_reduce_fusion.1
  418.5 0.1 reduce_sum.48
  418.6 0.0 copy-done.2
  418.6 0.1 copy.37
  418.7 0.1 select_reduce_fusion
  418.8 0.1 copy.38
  419.0 33.8 %all-to-all-done.2 = bf16[128,4,1024]{2,1,0:T(4,128)(2,1)} async-done(((bf16[128,4,1024]{2,1,0:T(4,128)(2,1)}), bf16[128,4,1024]{2,1,0:T(4,128)(2,1)}, u32[]{:S(2)}, u32[]{:S(2)}) %all-to-all-start.2) | async-done | bytes 1048608 | tf_op jit(solution)/shard_map/all_to_all | solution.py:76
  452.7 2.8 copy.62
  455.5 2.6 dot_general.24
  458.1 2.2 fusion.1
  (8 shorter events, 0.1 us)
Async XLA Ops:
  6.5 395.3 %copy-start = (bf16[2,768,1024]{2,1,0:T(8,128)(2,1)S(1)}, bf16[2,768,1024]{2,1,0:T(8,128)(2,1)}, u32[]{:S(2)}) copy-start(bf16[2,768,1024]{2,1,0:T(8,128)(2,1)} %param.13) | copy-start | bytes 9437188
  6.5 332.4 %all-gather.3.cloned.1.call-start = ((), (), s32[]{:S(2)}) async-start(), calls=%async_computation.3 | async-start | bytes 3244032 | tf_op jit(solution)/shard_map/all_gather | solution.py:43
  6.5 4.6 collective-permute-start
  345.0 3.6 copy-start.3
  348.6 1.9 copy-start.4
  402.9 15.0 %copy-start.1 = (s32[12,8]{0,1:T(8,128)S(1)}, s32[12,8]{0,1:T(8,128)}, u32[]{:S(2)}) copy-start(s32[12,8]{0,1:T(8,128)} %param.9) | copy-start | bytes 1156
  402.9 15.7 %copy-start.2 = (f32[12,8]{0,1:T(8,128)S(1)}, f32[12,8]{0,1:T(8,128)}, u32[]{:S(2)}) copy-start(f32[12,8]{0,1:T(8,128)} %param.10) | copy-start | bytes 1156
  404.7 48.0 %all-to-all-start.2 = ((bf16[128,4,1024]{2,1,0:T(4,128)(2,1)}), bf16[128,4,1024]{2,1,0:T(4,128)(2,1)}, u32[]{:S(2)}, u32[]{:S(2)}) async-start(bf16[128,4,1024]{2,1,0:T(4,128)(2,1)} %copy.47), calls=%async_computation.2 | async-start | bytes 2097152 | tf_op jit(solution)/shard_map/all_to_all | solution.py:76
Sparse Core Ops, SparseCore 0:
  25.9 144.3 all-gather.2

commit v5 on v2

--- a/solution.py
+++ b/solution.py
@@ -39,12 +39,12 @@
     )
     normed_parts = normed.reshape(tokens_here, dp_groups, width_part)
     send_rows = jnp.einsum(
-        "tes,tpw->epsw", occupied, normed_parts, preferred_element_type=jnp.float32
+        "tes,tpw->pesw", occupied, normed_parts, preferred_element_type=jnp.float32
     ).astype(jnp.bfloat16)
     devices = expert_groups * dp_groups
     outgoing = send_rows.reshape(devices, slot_rows, width_part)
     incoming = lax.all_to_all(
-        outgoing, ("expert", "dp"), split_axis=0, concat_axis=0, tiled=True
+        outgoing, ("dp", "expert"), split_axis=0, concat_axis=0, tiled=True
     )
     grouped = incoming.reshape(devices, experts_here, CAP, width_part)
     gate_part = jnp.einsum("nxcd,xdf->nxcf", grouped, w_gate, preferred_element_type=jnp.float32)
@@ -68,14 +68,14 @@
     ).astype(jnp.bfloat16)
     returning = expert_out.reshape(devices, slot_rows, width_part)
     returned = lax.all_to_all(
-        returning, ("expert", "dp"), split_axis=0, concat_axis=0, tiled=True
+        returning, ("dp", "expert"), split_axis=0, concat_axis=0, tiled=True
     )
-    back = returned.reshape(expert_groups, dp_groups, slot_rows, width_part)
+    back = returned.reshape(dp_groups, all_slots, width_part)
     weights = (gate_scores / jnp.sum(gate_scores, axis=-1, keepdims=True)).astype(jnp.bfloat16)
     combine = jnp.sum(
         jnp.where(placed, weights[:, :, None].astype(jnp.float32), 0.0), axis=1
-    ).astype(jnp.bfloat16).reshape(tokens_here, expert_groups, slot_rows)
-    mixed = jnp.einsum("tes,epsw->tpw", combine, back, preferred_element_type=jnp.float32)
+    ).astype(jnp.bfloat16)
+    mixed = jnp.einsum("tk,pkw->tpw", combine, back, preferred_element_type=jnp.float32)
     mixed_out = arrived_f + mixed.reshape(tokens_here, dp_groups * width_part)
     return mixed_out.astype(jnp.bfloat16)
 

time: 225 us -> 226 us (level)
  the two profiles are of different devices: /device:TPU:26 before, /device:TPU:18 now
where the time goes in v5:
time: 226 us; the launch traced here: 225 us
  blocking collectives  140 us (62%)
  waiting for transfers between devices  56.5 us (25%)
  starting transfers between devices  10.6 us (5%)
  local copies, waits for them, and re-layouts  9.72 us (4%)
  matrix products  5.74 us (3%)
    all_to_all x1, blocking collectives, per_device(): lax.all_to_all(outgoing, ('dp', 'expert'), split_axis=0, concat_axis=0, t...  82.9 us
    all_to_all x1, waiting for transfers between devices, per_device(): lax.all_to_all(returning, ('dp', 'expert'), split_axis=0, concat_axis=0,...  53.7 us
    all_to_all x1, blocking collectives, per_device(): lax.all_to_all(parts, 'dp', split_axis=0, concat_axis=0, tiled=False)  38.6 us
    all_gather x1, blocking collectives, per_device(): hidden = lax.all_gather(hidden_chunk, 'dp', axis=0, tiled=True)  18.9 us
    all_to_all x1, starting transfers between devices, per_device(): lax.all_to_all(returning, ('dp', 'expert'), split_axis=0, concat_axis=0,...  10.6 us
  transfers between devices with their start and end apart: 2, of which 2 were waited for; matrix products, arithmetic and copies ran while one was open for 1% of the time, Pallas kernels for 0%

profile of v5, /device:TPU:18, one launch (start us, length us, event | category | flops | bytes accessed | tf_op | source)
XLA Modules:
  0.0 225.2 jit_solution(1250777099575307018)
XLA Ops:
  0.0 0.0 copy-start
  0.0 0.0 collective-permute-start
  0.0 0.9 copy.32
  0.9 0.1 eq.29
  1.0 0.1 fusion.24
  1.1 0.1 reduce_window_sum.11
  1.2 0.2 select_reduce_fusion.1
  1.4 0.1 reduce_sum.48
  1.5 0.1 fusion.23
  1.6 0.1 copy.35
  1.8 0.1 copy.37
  1.9 2.7 %collective-permute-done = bf16[12,4096]{1,0:T(8,128)(2,1)S(1)} collective-permute-done((bf16[12,4096]{1,0:T(8,128)(2,1)}, bf16[12,4096]{1,0:T(8,128)(2,1)S(1)}, u32[]{:S(2)}, u32[]{:S(2)}) %collective-permute-start) | collective-permute-done | bytes 98336 | tf_op jit(solution)/shard_map/ppermute | solution.py:11
  4.6 0.1 fusion.19
  4.8 0.8 fusion.21
  5.6 0.1 reshape.51
  5.7 0.5 fusion.16
  6.2 0.1 copy.38
  6.3 0.0 copy-start.2
  6.3 0.8 copy.39
  7.1 82.9 %all_to_all.15 = bf16[128,4,1024]{2,1,0:T(4,128)(2,1)S(1)} all-to-all(bf16[128,4,1024]{2,1,0:T(4,128)(2,1)S(1)} %copy.39), channel_id=1, replica_groups=mesh['section'=8,'expert'=32,'dp'=4] {'dp','expert'}, dimensions={0} | all-to-all | bytes 2097152 | tf_op jit(solution)/shard_map/all_to_all | solution.py:46
  90.0 0.0 copy-start.3
  90.0 0.3 copy.40
  90.3 0.0 copy-done.2
  90.3 1.0 fusion.13
  91.3 0.6 copy-done.3
  91.9 1.0 fusion.10
  92.9 0.1 pad_maximum_fusion
  93.0 0.1 copy.51
  93.2 38.6 %all_to_all.16 = bf16[4,2,32,2,2,768]{5,2,4,3,1,0:T(8,128)(2,1)S(1)} all-to-all(bf16[4,2,32,2,2,768]{5,2,4,3,1,0:T(8,128)(2,1)S(1)} %copy.51), channel_id=1, replica_groups=mesh['section'=8,'expert'=32,'dp'=4] {'dp'}, dimensions={0} | all-to-all | bytes 3145728 | tf_op jit(solution)/shard_map/all_to_all | solution.py:60
  131.7 0.2 convert_reduce_fusion
  132.0 0.1 fusion.18
  132.1 18.9 %all_gather.3 = bf16[128,2,2,768]{3,0,2,1:T(8,128)(2,1)S(1)} all-gather(bf16[32,2,2,768]{3,0,2,1:T(8,128)(2,1)S(1)} %fusion.18), channel_id=1, replica_groups=mesh['section'=8,'expert'=32,'dp'=4] {'dp'}, dimensions={0}, use_global_device_ids=true | all-gather | bytes 983040 | tf_op jit(solution)/shard_map/all_gather | solution.py:64
  151.0 0.0 copy-done
  151.0 1.0 fusion.7
  152.0 0.0 copy-start.1
  152.0 1.8 copy.43
  153.9 10.6 %all-to-all-start.2 = ((bf16[128,4,1024]{2,1,0:T(4,128)(2,1)}), bf16[128,4,1024]{2,1,0:T(4,128)(2,1)}, u32[]{:S(2)}, u32[]{:S(2)}) async-start(bf16[128,4,1024]{2,1,0:T(4,128)(2,1)} %copy.43), calls=%async_computation.2 | async-start | bytes 2097152 | tf_op jit(solution)/shard_map/all_to_all | solution.py:70
  164.5 0.0 copy-done.1
  164.6 0.1 copy.34
  164.6 0.1 select_reduce_fusion
  164.7 53.7 %all-to-all-done.2 = bf16[128,4,1024]{2,1,0:T(4,128)(2,1)} async-done(((bf16[128,4,1024]{2,1,0:T(4,128)(2,1)}), bf16[128,4,1024]{2,1,0:T(4,128)(2,1)}, u32[]{:S(2)}, u32[]{:S(2)}) %all-to-all-start.2) | async-done | bytes 1048608 | tf_op jit(solution)/shard_map/all_to_all | solution.py:70
  218.5 2.2 reshape.56
  220.7 2.3 %copy.44 = bf16[4,1024,128]{2,1,0:T(8,128)(2,1)} copy(bf16[4,1024,128]{1,2,0:T(8,128)(2,1)} %bitcast.59) | data formatting | bytes 2097152 | tf_op jit(solution)/shard_map/tk,pkw->tpw/dot_general | solution.py:78
  223.0 2.3 %fusion = bf16[12,4096]{1,0:T(8,128)(2,1)} fusion(bf16[4096,128]{1,0:T(8,128)(2,1)} %bitcast.57, bf16[12,4096]{1,0:T(8,128)(2,1)S(1)} %collective-permute-done, bf16[12,128]{1,0:T(8,128)(2,1)S(1)} %select_reduce_fusion), kind=kOutput, calls=%fused_computation.1 | convolution fusion | flops 12730368 | bytes 1248256 | tf_op jit(solution)/shard_map/tk,pkw->tpw/dot_general | solution.py:78
  (4 shorter events, 0.0 us)
Async XLA Ops:
  0.0 151.0 %copy-start = (bf16[2,768,1024]{2,1,0:T(8,128)(2,1)S(1)}, bf16[2,768,1024]{2,1,0:T(8,128)(2,1)}, u32[]{:S(2)}) copy-start(bf16[2,768,1024]{2,1,0:T(8,128)(2,1)} %param.13) | copy-start | bytes 9437188
  0.0 4.6 %collective-permute-start = (bf16[12,4096]{1,0:T(8,128)(2,1)}, bf16[12,4096]{1,0:T(8,128)(2,1)S(1)}, u32[]{:S(2)}, u32[]{:S(2)}) collective-permute-start(bf16[12,4096]{1,0:T(8,128)(2,1)} %param.7), channel_id=1, source_target_pairs={{0,128},{128,256},{256,384},{384,512},{512,640},{640,768},{768,896... | collective-permute-start | bytes 294920 | tf_op jit(solution)/shard_map/ppermute | solution.py:11
  6.3 84.0 %copy-start.2 = (bf16[2,1024,768]{2,1,0:T(8,128)(2,1)S(1)}, bf16[2,1024,768]{2,1,0:T(8,128)(2,1)}, u32[]{:S(2)}) copy-start(bf16[2,1024,768]{2,1,0:T(8,128)(2,1)} %param.12) | copy-start | bytes 9437188
  90.0 1.9 copy-start.3
  152.0 12.5 %copy-start.1 = (f32[12,8]{0,1:T(8,128)S(1)}, f32[12,8]{0,1:T(8,128)}, u32[]{:S(2)}) copy-start(f32[12,8]{0,1:T(8,128)} %param.10) | copy-start | bytes 1156
  153.9 64.6 %all-to-all-start.2 = ((bf16[128,4,1024]{2,1,0:T(4,128)(2,1)}), bf16[128,4,1024]{2,1,0:T(4,128)(2,1)}, u32[]{:S(2)}, u32[]{:S(2)}) async-start(bf16[128,4,1024]{2,1,0:T(4,128)(2,1)} %copy.43), calls=%async_computation.2 | async-start | bytes 2097152 | tf_op jit(solution)/shard_map/all_to_all | solution.py:70

commit v6 on v3

--- a/solution.py
+++ b/solution.py
@@ -64,8 +64,11 @@
             ],
             axis=1,
         ).astype(jnp.bfloat16)
-        parts = lax.all_to_all(parts, "dp", split_axis=0, concat_axis=0, tiled=False)
-        summed = jnp.sum(parts.astype(jnp.float32), axis=0)
+        here = lax.axis_index("dp")
+        summed = lax.dynamic_index_in_dim(parts, here, 0, keepdims=False).astype(jnp.float32)
+        for shift in range(1, dp_groups):
+            piece = lax.dynamic_index_in_dim(parts, (here + shift) % dp_groups, 0, keepdims=False)
+            summed = summed + passed_along(piece, "dp", shift).astype(jnp.float32)
         hidden_chunk = (jax.nn.silu(summed[0]) * summed[1]).astype(jnp.bfloat16)
         hidden = lax.all_gather(hidden_chunk, "dp", axis=0, tiled=True)
         expert_out = jnp.einsum(

time: 251 us -> 247 us (0.984)
  starting transfers between devices: 58.9 us -> 95.3 us
  waiting for transfers between devices: 122 us -> 100 us
  blocking collectives: 46 us -> 30.3 us
    ppermute x1 -> x7, waiting for transfers between devices: 2.83 us -> 34.8 us  [passed_along(): lax.ppermute(shard, axis, [(i, (i + by) % peers) for i in range(peers)])]
    all_to_all x2, waiting for transfers between devices: 64.1 us -> 33.2 us  [per_device(): lax.all_to_all(outgoing, ('expert', 'dp'), split_axis=0, concat_axis=0, t...]
    ppermute x1 -> x7, starting transfers between devices: 0.01 us -> 29 us  [passed_along(): lax.ppermute(shard, axis, [(i, (i + by) % peers) for i in range(peers)])]
    all_gather x2, blocking collectives: 46 us -> 30.3 us  [per_device(): hidden = lax.all_gather(hidden_chunk, 'dp', axis=0, tiled=True)]
    all_to_all x2, starting transfers between devices: 20.1 us -> 34.5 us  [per_device(): lax.all_to_all(expert_out, ('expert', 'dp'), split_axis=0, concat_axis=0,...]
    all_to_all x2 -> x0, waiting for transfers between devices: 13.9 us -> none  [per_device(): lax.all_to_all(parts, 'dp', split_axis=0, concat_axis=0, tiled=False)]
    all_to_all x2, waiting for transfers between devices: 41.2 us -> 32.4 us  [per_device(): lax.all_to_all(expert_out, ('expert', 'dp'), split_axis=0, concat_axis=0,...]
    all_to_all x2 -> x0, starting transfers between devices: 6.99 us -> none  [per_device(): lax.all_to_all(parts, 'dp', split_axis=0, concat_axis=0, tiled=False)]
  transfers between devices with their start and end apart: 7 -> 11, of which waited for: 6 -> 9; matrix products, arithmetic and copies ran while one was open for 8% -> 6% of each run, Pallas kernels for 0% -> 0%
where the time goes in v6:
time: 247 us; the launch traced here: 246 us
  waiting for transfers between devices  100 us (40%)
  starting transfers between devices  95.3 us (39%)
  blocking collectives  30.3 us (12%)
  matrix products  9.34 us (4%)
  local copies, waits for them, and re-layouts  7.87 us (3%)
  other arithmetic  2.77 us (1%)
    ppermute x7, waiting for transfers between devices, passed_along(): lax.ppermute(shard, axis, [(i, (i + by) % peers) for i in range(peers)])  34.8 us
    all_to_all x2, starting transfers between devices, per_device(): lax.all_to_all(expert_out, ('expert', 'dp'), split_axis=0, concat_axis=0,...  34.5 us
    all_to_all x2, waiting for transfers between devices, per_device(): lax.all_to_all(outgoing, ('expert', 'dp'), split_axis=0, concat_axis=0, t...  33.2 us
    all_to_all x2, waiting for transfers between devices, per_device(): lax.all_to_all(expert_out, ('expert', 'dp'), split_axis=0, concat_axis=0,...  32.4 us
    all_to_all x2, starting transfers between devices, per_device(): lax.all_to_all(outgoing, ('expert', 'dp'), split_axis=0, concat_axis=0, t...  31.8 us
    all_gather x2, blocking collectives, per_device(): hidden = lax.all_gather(hidden_chunk, 'dp', axis=0, tiled=True)  30.3 us
    ppermute x7, starting transfers between devices, passed_along(): lax.ppermute(shard, axis, [(i, (i + by) % peers) for i in range(peers)])  29 us
  transfers between devices with their start and end apart: 11, of which 9 were waited for; matrix products, arithmetic and copies ran while one was open for 6% of the time, Pallas kernels for 0%

profile of v6, /device:TPU:10, one launch (start us, length us, event | category | flops | bytes accessed | tf_op | source)
XLA Modules:
  0.0 246.4 jit_solution(12312414700954392022)
XLA Ops:
  0.0 0.8 copy.70
  0.8 0.1 eq.36
  0.9 0.1 fusion.86
  0.9 0.1 reduce_window_sum.11
  1.1 0.2 select_reduce_fusion.1
  1.3 0.1 reduce_sum.39
  1.4 0.1 fusion.85
  1.5 0.1 copy.75
  1.7 0.1 copy.77
  1.8 2.8 %collective-permute-done = bf16[12,4096]{1,0:T(8,128)(2,1)S(1)} collective-permute-done((bf16[12,4096]{1,0:T(8,128)(2,1)}, bf16[12,4096]{1,0:T(8,128)(2,1)S(1)}, u32[]{:S(2)}, u32[]{:S(2)}) %collective-permute-start) | collective-permute-done | bytes 98336 | tf_op jit(solution)/shard_map/ppermute | solution.py:11
  4.6 0.1 fusion.60
  4.8 0.8 fusion.62
  5.6 0.1 reshape.77
  5.7 0.5 fusion.18
  6.2 0.1 fusion.91
  6.3 1.3 copy.78
  7.6 25.8 %all-to-all-start = ((bf16[128,2,1024]{2,1,0:T(2,128)(2,1)}), bf16[128,2,1024]{2,1,0:T(2,128)(2,1)S(1)}, u32[]{:S(2)}, u32[]{:S(2)}) async-start(bf16[128,2,1024]{2,1,0:T(2,128)(2,1)} %bitcast.6), calls=%async_computation | async-start | bytes 1048576 | tf_op jit(solution)/shard_map/all_to_all | solution.py:53
  33.4 1.3 copy.85
  34.7 33.2 %all-to-all-done = bf16[128,2,1024]{2,1,0:T(2,128)(2,1)S(1)} async-done(((bf16[128,2,1024]{2,1,0:T(2,128)(2,1)}), bf16[128,2,1024]{2,1,0:T(2,128)(2,1)S(1)}, u32[]{:S(2)}, u32[]{:S(2)}) %all-to-all-start) | async-done | bytes 524320 | tf_op jit(solution)/shard_map/all_to_all | solution.py:53
  67.9 6.0 %all-to-all-start.2 = ((bf16[128,2,1024]{2,1,0:T(2,128)(2,1)}), bf16[128,2,1024]{2,1,0:T(2,128)(2,1)S(1)}, u32[]{:S(2)}, u32[]{:S(2)}) async-start(bf16[128,2,1024]{2,1,0:T(2,128)(2,1)} %bitcast.29), calls=%async_computation.2 | async-start | bytes 1048576 | tf_op jit(solution)/shard_map/all_to_all | solution.py:53
  74.0 0.1 copy.79
  74.1 2.1 fusion.43
  76.3 0.1 copy-done.1
  76.3 0.6 fusion.46
  76.9 0.1 fusion.77
  77.0 4.3 %collective-permute-start.1 = (bf16[2,32,2,768]{3,1,2,0:T(8,128)(2,1)S(1)}, bf16[2,32,2,768]{3,1,2,0:T(8,128)(2,1)S(1)}, u32[]{:S(2)}, u32[]{:S(2)}) collective-permute-start(bf16[2,32,2,768]{3,1,2,0:T(8,128)(2,1)S(1)} %get-tuple-element.10), channel_id=1, source_target_pairs={{0,1},{1,2},{2,3},{3,0},{4,5},{5,6},{6,7},{7,4},{8,9},{9,10},{10,1... | collective-permute-start | bytes 589832 | tf_op jit(solution)/shard_map/ppermute | solution.py:11
  81.3 4.6 %collective-permute-start.2 = (bf16[2,32,2,768]{3,1,2,0:T(8,128)(2,1)S(1)}, bf16[2,32,2,768]{3,1,2,0:T(8,128)(2,1)S(1)}, u32[]{:S(2)}, u32[]{:S(2)}) collective-permute-start(bf16[2,32,2,768]{3,1,2,0:T(8,128)(2,1)S(1)} %get-tuple-element.11), channel_id=1, source_target_pairs={{0,2},{1,3},{2,0},{3,1},{4,6},{5,7},{6,4},{7,5},{8,10},{9,11},{10,... | collective-permute-start | bytes 589832 | tf_op jit(solution)/shard_map/ppermute | solution.py:11
  85.9 5.5 %collective-permute-start.3 = (bf16[2,32,2,768]{3,1,2,0:T(8,128)(2,1)S(1)}, bf16[2,32,2,768]{3,1,2,0:T(8,128)(2,1)S(1)}, u32[]{:S(2)}, u32[]{:S(2)}) collective-permute-start(bf16[2,32,2,768]{3,1,2,0:T(8,128)(2,1)S(1)} %get-tuple-element.12), channel_id=1, source_target_pairs={{0,3},{1,0},{2,1},{3,2},{4,7},{5,4},{6,5},{7,6},{8,11},{9,8},{10,9... | collective-permute-start | bytes 589832 | tf_op jit(solution)/shard_map/ppermute | solution.py:11
  91.3 4.9 %collective-permute-done.1 = bf16[2,32,2,768]{3,1,2,0:T(8,128)(2,1)S(1)} collective-permute-done((bf16[2,32,2,768]{3,1,2,0:T(8,128)(2,1)S(1)}, bf16[2,32,2,768]{3,1,2,0:T(8,128)(2,1)S(1)}, u32[]{:S(2)}, u32[]{:S(2)}) %collective-permute-start.1) | collective-permute-done | bytes 196640 | tf_op jit(solution)/shard_map/ppermute | solution.py:11
  96.2 9.1 %collective-permute-done.2 = bf16[2,32,2,768]{3,1,2,0:T(8,128)(2,1)S(1)} collective-permute-done((bf16[2,32,2,768]{3,1,2,0:T(8,128)(2,1)S(1)}, bf16[2,32,2,768]{3,1,2,0:T(8,128)(2,1)S(1)}, u32[]{:S(2)}, u32[]{:S(2)}) %collective-permute-start.2) | collective-permute-done | bytes 196640 | tf_op jit(solution)/shard_map/ppermute | solution.py:11
  105.4 3.0 %collective-permute-done.3 = bf16[2,32,2,768]{3,1,2,0:T(8,128)(2,1)S(1)} collective-permute-done((bf16[2,32,2,768]{3,1,2,0:T(8,128)(2,1)S(1)}, bf16[2,32,2,768]{3,1,2,0:T(8,128)(2,1)S(1)}, u32[]{:S(2)}, u32[]{:S(2)}) %collective-permute-start.3) | collective-permute-done | bytes 196640 | tf_op jit(solution)/shard_map/ppermute | solution.py:11
  108.3 0.1 fusion.59
  108.4 0.1 fusion.83
  108.5 15.0 %all_gather.6 = bf16[128,2,768]{2,0,1:T(8,128)(2,1)S(1)} all-gather(bf16[32,2,768]{2,0,1:T(8,128)(2,1)S(1)} %fusion.83), channel_id=1, replica_groups=mesh['section'=8,'expert'=32,'dp'=4] {'dp'}, dimensions={0}, use_global_device_ids=true | all-gather | bytes 491520 | tf_op jit(solution)/shard_map/all_gather | solution.py:73
  123.4 2.0 fusion.19
  125.5 1.3 copy.82
  126.8 17.3 %all-to-all-start.1 = ((bf16[128,2,1024]{2,1,0:T(2,128)(2,1)}), bf16[128,2,1024]{2,1,0:T(2,128)(2,1)S(1)}, u32[]{:S(2)}, u32[]{:S(2)}) async-start(bf16[128,2,1024]{2,1,0:T(2,128)(2,1)} %copy.82), calls=%async_computation.1 | async-start | bytes 1048576 | tf_op jit(solution)/shard_map/all_to_all | solution.py:77
  144.1 0.1 copy.86
  144.2 2.1 fusion.37
  146.3 0.1 copy-done.2
  146.4 0.6 fusion.40
  147.1 4.4 %collective-permute-start.4 = (bf16[2,32,2,768]{3,1,2,0:T(8,128)(2,1)S(1)}, bf16[2,32,2,768]{3,1,2,0:T(8,128)(2,1)S(1)}, u32[]{:S(2)}, u32[]{:S(2)}) collective-permute-start(bf16[2,32,2,768]{3,1,2,0:T(8,128)(2,1)S(1)} %get-tuple-element.7), channel_id=1, source_target_pairs={{0,1},{1,2},{2,3},{3,0},{4,5},{5,6},{6,7},{7,4},{8,9},{9,10},{10,1... | collective-permute-start | bytes 589832 | tf_op jit(solution)/shard_map/ppermute | solution.py:11
  151.5 4.6 %collective-permute-start.5 = (bf16[2,32,2,768]{3,1,2,0:T(8,128)(2,1)S(1)}, bf16[2,32,2,768]{3,1,2,0:T(8,128)(2,1)S(1)}, u32[]{:S(2)}, u32[]{:S(2)}) collective-permute-start(bf16[2,32,2,768]{3,1,2,0:T(8,128)(2,1)S(1)} %get-tuple-element.8), channel_id=1, source_target_pairs={{0,2},{1,3},{2,0},{3,1},{4,6},{5,7},{6,4},{7,5},{8,10},{9,11},{10,... | collective-permute-start | bytes 589832 | tf_op jit(solution)/shard_map/ppermute | solution.py:11
  156.1 5.7 %collective-permute-start.6 = (bf16[2,32,2,768]{3,1,2,0:T(8,128)(2,1)S(1)}, bf16[2,32,2,768]{3,1,2,0:T(8,128)(2,1)S(1)}, u32[]{:S(2)}, u32[]{:S(2)}) collective-permute-start(bf16[2,32,2,768]{3,1,2,0:T(8,128)(2,1)S(1)} %get-tuple-element.9), channel_id=1, source_target_pairs={{0,3},{1,0},{2,1},{3,2},{4,7},{5,4},{6,5},{7,6},{8,11},{9,8},{10,9... | collective-permute-start | bytes 589832 | tf_op jit(solution)/shard_map/ppermute | solution.py:11
  161.8 2.8 %collective-permute-done.4 = bf16[2,32,2,768]{3,1,2,0:T(8,128)(2,1)S(1)} collective-permute-done((bf16[2,32,2,768]{3,1,2,0:T(8,128)(2,1)S(1)}, bf16[2,32,2,768]{3,1,2,0:T(8,128)(2,1)S(1)}, u32[]{:S(2)}, u32[]{:S(2)}) %collective-permute-start.4) | collective-permute-done | bytes 196640 | tf_op jit(solution)/shard_map/ppermute | solution.py:11
  164.6 10.8 %collective-permute-done.5 = bf16[2,32,2,768]{3,1,2,0:T(8,128)(2,1)S(1)} collective-permute-done((bf16[2,32,2,768]{3,1,2,0:T(8,128)(2,1)S(1)}, bf16[2,32,2,768]{3,1,2,0:T(8,128)(2,1)S(1)}, u32[]{:S(2)}, u32[]{:S(2)}) %collective-permute-start.5) | collective-permute-done | bytes 196640 | tf_op jit(solution)/shard_map/ppermute | solution.py:11
  175.4 1.4 collective-permute-done.6
  176.8 0.1 fusion.57
  176.9 0.1 fusion.81
  177.0 15.3 %all_gather.7 = bf16[128,2,768]{2,0,1:T(8,128)(2,1)S(1)} all-gather(bf16[32,2,768]{2,0,1:T(8,128)(2,1)S(1)} %fusion.81), channel_id=1, replica_groups=mesh['section'=8,'expert'=32,'dp'=4] {'dp'}, dimensions={0}, use_global_device_ids=true | all-gather | bytes 491520 | tf_op jit(solution)/shard_map/all_gather | solution.py:73
  192.3 0.6 fusion.22
  192.9 1.3 copy.89
  194.2 17.2 %all-to-all-start.3 = ((bf16[128,2,1024]{2,1,0:T(2,128)(2,1)}), bf16[128,2,1024]{2,1,0:T(2,128)(2,1)S(1)}, u32[]{:S(2)}, u32[]{:S(2)}) async-start(bf16[128,2,1024]{2,1,0:T(2,128)(2,1)} %copy.89), calls=%async_computation.3 | async-start | bytes 1048576 | tf_op jit(solution)/shard_map/all_to_all | solution.py:77
  211.5 0.1 copy.72
  211.6 0.1 select_reduce_fusion
  211.7 0.1 copy.73
  211.9 0.1 copy.101
  212.0 0.1 copy.102
  212.1 0.4 convolution_bitcast_fusion.1
  212.5 32.4 %all-to-all-done.3 = bf16[128,2,1024]{2,1,0:T(2,128)(2,1)S(1)} async-done(((bf16[128,2,1024]{2,1,0:T(2,128)(2,1)}), bf16[128,2,1024]{2,1,0:T(2,128)(2,1)S(1)}, u32[]{:S(2)}, u32[]{:S(2)}) %all-to-all-start.3) | async-done | bytes 524320 | tf_op jit(solution)/shard_map/all_to_all | solution.py:77
  244.9 0.4 fusion.49
  245.3 0.1 copy.91
  245.5 0.2 copy.103
  245.7 0.7 fusion.63
  (17 shorter events, 0.2 us)
Async XLA Ops:
  0.0 4.6 %collective-permute-start = (bf16[12,4096]{1,0:T(8,128)(2,1)}, bf16[12,4096]{1,0:T(8,128)(2,1)S(1)}, u32[]{:S(2)}, u32[]{:S(2)}) collective-permute-start(bf16[12,4096]{1,0:T(8,128)(2,1)} %param.7), channel_id=1, source_target_pairs={{0,128},{128,256},{256,384},{384,512},{512,640},{640,768},{768,896... | collective-permute-start | bytes 294920 | tf_op jit(solution)/shard_map/ppermute | solution.py:11
  7.6 60.3 %all-to-all-start = ((bf16[128,2,1024]{2,1,0:T(2,128)(2,1)}), bf16[128,2,1024]{2,1,0:T(2,128)(2,1)S(1)}, u32[]{:S(2)}, u32[]{:S(2)}) async-start(bf16[128,2,1024]{2,1,0:T(2,128)(2,1)} %bitcast.6), calls=%async_computation | async-start | bytes 1048576 | tf_op jit(solution)/shard_map/all_to_all | solution.py:53
  67.9 58.9 %all-to-all-start.2 = ((bf16[128,2,1024]{2,1,0:T(2,128)(2,1)}), bf16[128,2,1024]{2,1,0:T(2,128)(2,1)S(1)}, u32[]{:S(2)}, u32[]{:S(2)}) async-start(bf16[128,2,1024]{2,1,0:T(2,128)(2,1)} %bitcast.29), calls=%async_computation.2 | async-start | bytes 1048576 | tf_op jit(solution)/shard_map/all_to_all | solution.py:53
  74.0 2.4 copy-start.1
  77.0 19.2 %collective-permute-start.1 = (bf16[2,32,2,768]{3,1,2,0:T(8,128)(2,1)S(1)}, bf16[2,32,2,768]{3,1,2,0:T(8,128)(2,1)S(1)}, u32[]{:S(2)}, u32[]{:S(2)}) collective-permute-start(bf16[2,32,2,768]{3,1,2,0:T(8,128)(2,1)S(1)} %get-tuple-element.10), channel_id=1, source_target_pairs={{0,1},{1,2},{2,3},{3,0},{4,5},{5,6},{6,7},{7,4},{8,9},{9,10},{10,1... | collective-permute-start | bytes 589832 | tf_op jit(solution)/shard_map/ppermute | solution.py:11
  81.3 24.1 %collective-permute-start.2 = (bf16[2,32,2,768]{3,1,2,0:T(8,128)(2,1)S(1)}, bf16[2,32,2,768]{3,1,2,0:T(8,128)(2,1)S(1)}, u32[]{:S(2)}, u32[]{:S(2)}) collective-permute-start(bf16[2,32,2,768]{3,1,2,0:T(8,128)(2,1)S(1)} %get-tuple-element.11), channel_id=1, source_target_pairs={{0,2},{1,3},{2,0},{3,1},{4,6},{5,7},{6,4},{7,5},{8,10},{9,11},{10,... | collective-permute-start | bytes 589832 | tf_op jit(solution)/shard_map/ppermute | solution.py:11
  85.9 22.4 %collective-permute-start.3 = (bf16[2,32,2,768]{3,1,2,0:T(8,128)(2,1)S(1)}, bf16[2,32,2,768]{3,1,2,0:T(8,128)(2,1)S(1)}, u32[]{:S(2)}, u32[]{:S(2)}) collective-permute-start(bf16[2,32,2,768]{3,1,2,0:T(8,128)(2,1)S(1)} %get-tuple-element.12), channel_id=1, source_target_pairs={{0,3},{1,0},{2,1},{3,2},{4,7},{5,4},{6,5},{7,6},{8,11},{9,8},{10,9... | collective-permute-start | bytes 589832 | tf_op jit(solution)/shard_map/ppermute | solution.py:11
  126.8 67.5 %all-to-all-start.1 = ((bf16[128,2,1024]{2,1,0:T(2,128)(2,1)}), bf16[128,2,1024]{2,1,0:T(2,128)(2,1)S(1)}, u32[]{:S(2)}, u32[]{:S(2)}) async-start(bf16[128,2,1024]{2,1,0:T(2,128)(2,1)} %copy.82), calls=%async_computation.1 | async-start | bytes 1048576 | tf_op jit(solution)/shard_map/all_to_all | solution.py:77
  144.1 2.4 copy-start.2
  146.4 45.9 %copy-start.3 = (bf16[2,768,1024]{2,1,0:T(8,128)(2,1)S(1)}, bf16[2,768,1024]{2,1,0:T(8,128)(2,1)}, u32[]{:S(2)}) copy-start(bf16[2,768,1024]{2,1,0:T(8,128)(2,1)} %param.13) | copy-start | bytes 9437188
  147.1 17.5 %collective-permute-start.4 = (bf16[2,32,2,768]{3,1,2,0:T(8,128)(2,1)S(1)}, bf16[2,32,2,768]{3,1,2,0:T(8,128)(2,1)S(1)}, u32[]{:S(2)}, u32[]{:S(2)}) collective-permute-start(bf16[2,32,2,768]{3,1,2,0:T(8,128)(2,1)S(1)} %get-tuple-element.7), channel_id=1, source_target_pairs={{0,1},{1,2},{2,3},{3,0},{4,5},{5,6},{6,7},{7,4},{8,9},{9,10},{10,1... | collective-permute-start | bytes 589832 | tf_op jit(solution)/shard_map/ppermute | solution.py:11
  151.5 23.9 %collective-permute-start.5 = (bf16[2,32,2,768]{3,1,2,0:T(8,128)(2,1)S(1)}, bf16[2,32,2,768]{3,1,2,0:T(8,128)(2,1)S(1)}, u32[]{:S(2)}, u32[]{:S(2)}) collective-permute-start(bf16[2,32,2,768]{3,1,2,0:T(8,128)(2,1)S(1)} %get-tuple-element.8), channel_id=1, source_target_pairs={{0,2},{1,3},{2,0},{3,1},{4,6},{5,7},{6,4},{7,5},{8,10},{9,11},{10,... | collective-permute-start | bytes 589832 | tf_op jit(solution)/shard_map/ppermute | solution.py:11
  156.1 20.7 %collective-permute-start.6 = (bf16[2,32,2,768]{3,1,2,0:T(8,128)(2,1)S(1)}, bf16[2,32,2,768]{3,1,2,0:T(8,128)(2,1)S(1)}, u32[]{:S(2)}, u32[]{:S(2)}) collective-permute-start(bf16[2,32,2,768]{3,1,2,0:T(8,128)(2,1)S(1)} %get-tuple-element.9), channel_id=1, source_target_pairs={{0,3},{1,0},{2,1},{3,2},{4,7},{5,4},{6,5},{7,6},{8,11},{9,8},{10,9... | collective-permute-start | bytes 589832 | tf_op jit(solution)/shard_map/ppermute | solution.py:11
  176.9 34.6 %copy-start = (f32[12,8]{0,1:T(8,128)S(1)}, f32[12,8]{0,1:T(8,128)}, u32[]{:S(2)}) copy-start(f32[12,8]{0,1:T(8,128)} %param.10) | copy-start | bytes 1156
  194.2 50.7 %all-to-all-start.3 = ((bf16[128,2,1024]{2,1,0:T(2,128)(2,1)}), bf16[128,2,1024]{2,1,0:T(2,128)(2,1)S(1)}, u32[]{:S(2)}, u32[]{:S(2)}) async-start(bf16[128,2,1024]{2,1,0:T(2,128)(2,1)} %copy.89), calls=%async_computation.3 | async-start | bytes 1048576 | tf_op jit(solution)/shard_map/all_to_all | solution.py:77

commit v7 on v3

--- a/solution.py
+++ b/solution.py
@@ -57,16 +57,10 @@
             "ncd,df->ncf", grouped, w_gate[x], preferred_element_type=jnp.float32
         )
         up_part = jnp.einsum("ncd,df->ncf", grouped, w_up[x], preferred_element_type=jnp.float32)
-        parts = jnp.stack(
-            [
-                gate_part.reshape(dp_groups, chunks, CAP, -1),
-                up_part.reshape(dp_groups, chunks, CAP, -1),
-            ],
-            axis=1,
-        ).astype(jnp.bfloat16)
-        parts = lax.all_to_all(parts, "dp", split_axis=0, concat_axis=0, tiled=False)
-        summed = jnp.sum(parts.astype(jnp.float32), axis=0)
-        hidden_chunk = (jax.nn.silu(summed[0]) * summed[1]).astype(jnp.bfloat16)
+        parts = jnp.stack([gate_part, up_part], axis=1).astype(jnp.bfloat16)
+        summed = lax.psum_scatter(parts, "dp", scatter_dimension=0, tiled=True)
+        summed = summed.astype(jnp.float32)
+        hidden_chunk = (jax.nn.silu(summed[:, 0]) * summed[:, 1]).astype(jnp.bfloat16)
         hidden = lax.all_gather(hidden_chunk, "dp", axis=0, tiled=True)
         expert_out = jnp.einsum(
             "ncf,fd->ncd", hidden, w_down[x], preferred_element_type=jnp.float32

time: 251 us -> 250 us (level)
  between operations: 0.29 us -> 13.6 us
  blocking collectives: 46 us -> 33.7 us
  waiting for transfers between devices: 122 us -> 110 us
  starting transfers between devices: 58.9 us -> 68.2 us
  other arithmetic: 2.81 us -> 6.27 us
    all_to_all x2, starting transfers between devices: 20.1 us -> 36.3 us  [per_device(): lax.all_to_all(expert_out, ('expert', 'dp'), split_axis=0, concat_axis=0,...]
    all_to_all x2 -> x0, waiting for transfers between devices: 13.9 us -> none  [per_device(): lax.all_to_all(parts, 'dp', split_axis=0, concat_axis=0, tiled=False)]
    all_gather x2, blocking collectives: 46 us -> 33.7 us  [per_device(): hidden = lax.all_gather(hidden_chunk, 'dp', axis=0, tiled=True)]
    reduce_scatter x0 -> x2, waiting for transfers between devices: none -> 11.1 us  [per_device(): summed = lax.psum_scatter(parts, 'dp', scatter_dimension=0, tiled=True)]
    all_to_all x2, waiting for transfers between devices: 41.2 us -> 32.5 us  [per_device(): lax.all_to_all(expert_out, ('expert', 'dp'), split_axis=0, concat_axis=0,...]
    all_to_all x2 -> x0, starting transfers between devices: 6.99 us -> none  [per_device(): lax.all_to_all(parts, 'dp', split_axis=0, concat_axis=0, tiled=False)]
  transfers between devices with their start and end apart: 7 -> 7, of which waited for: 6 -> 7; matrix products, arithmetic and copies ran while one was open for 8% -> 8% of each run, Pallas kernels for 0% -> 0%
where the time goes in v7:
time: 250 us
  waiting for transfers between devices  110 us (44%)
  starting transfers between devices  68.2 us (27%)
  blocking collectives  33.7 us (13%)
  between operations  13.6 us (5%)
  matrix products  9.39 us (4%)
  local copies, waits for them, and re-layouts  7.94 us (3%)
  other arithmetic  6.27 us (3%)
    all_to_all x2, waiting for transfers between devices, per_device(): lax.all_to_all(outgoing, ('expert', 'dp'), split_axis=0, concat_axis=0, t...  64 us
    all_to_all x2, starting transfers between devices, per_device(): lax.all_to_all(expert_out, ('expert', 'dp'), split_axis=0, concat_axis=0,...  36.3 us
    all_gather x2, blocking collectives, per_device(): hidden = lax.all_gather(hidden_chunk, 'dp', axis=0, tiled=True)  33.7 us
    all_to_all x2, waiting for transfers between devices, per_device(): lax.all_to_all(expert_out, ('expert', 'dp'), split_axis=0, concat_axis=0,...  32.5 us
    all_to_all x2, starting transfers between devices, per_device(): lax.all_to_all(outgoing, ('expert', 'dp'), split_axis=0, concat_axis=0, t...  31.8 us
    reduce_scatter x2, waiting for transfers between devices, per_device(): summed = lax.psum_scatter(parts, 'dp', scatter_dimension=0, tiled=True)  11.1 us
  transfers between devices with their start and end apart: 7, of which 7 were waited for; matrix products, arithmetic and copies ran while one was open for 8% of the time, Pallas kernels for 0%

profile of v7, /device:TPU:10, one launch (start us, length us, event | category | flops | bytes accessed | tf_op | source)
XLA Modules:
  0.0 249.6 jit_solution(17952799181074950070)
XLA Ops:
  6.5 0.0 collective-permute-start
  6.5 0.8 copy.62
  7.3 0.1 eq.29
  7.4 0.1 fusion.66
  7.5 0.1 reduce_window_sum.11
  7.6 0.2 select_reduce_fusion.1
  7.8 0.1 reduce_sum.39
  7.9 0.1 fusion.65
  8.0 0.1 copy.67
  8.2 0.1 copy.69
  8.3 2.8 %collective-permute-done = bf16[12,4096]{1,0:T(8,128)(2,1)S(1)} collective-permute-done((bf16[12,4096]{1,0:T(8,128)(2,1)}, bf16[12,4096]{1,0:T(8,128)(2,1)S(1)}, u32[]{:S(2)}, u32[]{:S(2)}) %collective-permute-start) | collective-permute-done | bytes 98336 | tf_op jit(solution)/shard_map/ppermute | solution.py:11
  11.1 0.1 fusion.56
  11.3 0.8 fusion.58
  12.1 0.1 reshape.49
  12.2 0.5 fusion.18
  12.7 0.1 fusion.71
  12.8 1.3 copy.70
  14.1 25.8 %all-to-all-start = ((bf16[128,2,1024]{2,1,0:T(2,128)(2,1)}), bf16[128,2,1024]{2,1,0:T(2,128)(2,1)S(1)}, u32[]{:S(2)}, u32[]{:S(2)}) async-start(bf16[128,2,1024]{2,1,0:T(2,128)(2,1)} %bitcast.6), calls=%async_computation | async-start | bytes 1048576 | tf_op jit(solution)/shard_map/all_to_all | solution.py:53
  39.9 1.3 copy.76
  41.3 33.2 %all-to-all-done = bf16[128,2,1024]{2,1,0:T(2,128)(2,1)S(1)} async-done(((bf16[128,2,1024]{2,1,0:T(2,128)(2,1)}), bf16[128,2,1024]{2,1,0:T(2,128)(2,1)S(1)}, u32[]{:S(2)}, u32[]{:S(2)}) %all-to-all-start) | async-done | bytes 524320 | tf_op jit(solution)/shard_map/all_to_all | solution.py:53
  74.5 6.0 %all-to-all-start.2 = ((bf16[128,2,1024]{2,1,0:T(2,128)(2,1)}), bf16[128,2,1024]{2,1,0:T(2,128)(2,1)S(1)}, u32[]{:S(2)}, u32[]{:S(2)}) async-start(bf16[128,2,1024]{2,1,0:T(2,128)(2,1)} %bitcast.22), calls=%async_computation.3 | async-start | bytes 1048576 | tf_op jit(solution)/shard_map/all_to_all | solution.py:53
  80.5 0.0 reduce-scatter.3.cloned.1.call-start
  80.5 0.0 copy-start.1
  80.5 2.1 fusion.43
  82.7 0.2 copy-done.1
  82.9 0.6 fusion.46
  83.5 0.9 pad_maximum_fusion
  84.4 0.0 reduce-scatter.3.cloned.1.call-update
  84.5 0.0 reduce-scatter.5.cloned.1.call-start
  84.5 30.8 %all-to-all-done.2 = bf16[128,2,1024]{2,1,0:T(2,128)(2,1)S(1)} async-done(((bf16[128,2,1024]{2,1,0:T(2,128)(2,1)}), bf16[128,2,1024]{2,1,0:T(2,128)(2,1)S(1)}, u32[]{:S(2)}, u32[]{:S(2)}) %all-to-all-start.2) | async-done | bytes 524320 | tf_op jit(solution)/shard_map/all_to_all | solution.py:53
  115.3 2.1 fusion.37
  117.5 0.2 copy-done.2
  117.7 0.6 fusion.40
  118.3 0.0 copy-start.3
  118.3 1.0 pad_maximum_fusion.1
  119.3 0.0 reduce-scatter.5.cloned.1.call-update
  119.3 3.9 %reduce-scatter.3.cloned.1.call-done = bf16[32,2,2,768]{3,0,2,1:T(8,128)(2,1)} async-done(((bf16[128,2,2,768]{3,0,2,1:T(8,128)(2,1)}), bf16[32,2,2,768]{3,0,2,1:T(8,128)(2,1)}) %reduce-scatter.3.cloned.1.call-update) | async-done | bytes 196624 | tf_op jit(solution)/shard_map/reduce_scatter | solution.py:61
  123.2 1.0 convert_element_type.62
  124.2 0.1 fusion.63
  124.3 15.2 %all_gather.6 = bf16[128,2,768]{2,0,1:T(8,128)(2,1)S(1)} all-gather(bf16[32,2,768]{2,0,1:T(8,128)(2,1)S(1)} %fusion.63), channel_id=1, replica_groups=mesh['section'=8,'expert'=32,'dp'=4] {'dp'}, dimensions={0}, use_global_device_ids=true | all-gather | bytes 491520 | tf_op jit(solution)/shard_map/all_gather | solution.py:64
  139.5 0.0 copy-done.3
  139.5 0.6 fusion.19
  140.0 1.3 copy.73
  141.4 17.8 %all-to-all-start.1 = ((bf16[128,2,1024]{2,1,0:T(2,128)(2,1)}), bf16[128,2,1024]{2,1,0:T(2,128)(2,1)S(1)}, u32[]{:S(2)}, u32[]{:S(2)}) async-start(bf16[128,2,1024]{2,1,0:T(2,128)(2,1)} %copy.73), calls=%async_computation.2 | async-start | bytes 1048576 | tf_op jit(solution)/shard_map/all_to_all | solution.py:68
  159.2 7.1 %reduce-scatter.5.cloned.1.call-done = bf16[32,2,2,768]{3,0,2,1:T(8,128)(2,1)} async-done(((bf16[128,2,2,768]{3,0,2,1:T(8,128)(2,1)}), bf16[32,2,2,768]{3,0,2,1:T(8,128)(2,1)}) %reduce-scatter.5.cloned.1.call-update) | async-done | bytes 196624 | tf_op jit(solution)/shard_map/reduce_scatter | solution.py:61
  166.3 1.0 convert_element_type.65
  167.3 0.0 copy-start
  167.3 0.1 fusion.61
  167.4 18.5 %all_gather.7 = bf16[128,2,768]{2,0,1:T(8,128)(2,1)S(1)} all-gather(bf16[32,2,768]{2,0,1:T(8,128)(2,1)S(1)} %fusion.61), channel_id=1, replica_groups=mesh['section'=8,'expert'=32,'dp'=4] {'dp'}, dimensions={0}, use_global_device_ids=true | all-gather | bytes 491520 | tf_op jit(solution)/shard_map/all_gather | solution.py:64
  185.9 2.0 fusion.22
  187.9 1.4 copy.79
  189.3 1.1 all-to-all-done.1
  190.4 18.5 %all-to-all-start.3 = ((bf16[128,2,1024]{2,1,0:T(2,128)(2,1)}), bf16[128,2,1024]{2,1,0:T(2,128)(2,1)S(1)}, u32[]{:S(2)}, u32[]{:S(2)}) async-start(bf16[128,2,1024]{2,1,0:T(2,128)(2,1)} %copy.79), calls=%async_computation.5 | async-start | bytes 1048576 | tf_op jit(solution)/shard_map/all_to_all | solution.py:68
  208.9 0.1 copy.64
  209.0 0.1 select_reduce_fusion
  209.1 0.1 copy.65
  209.3 0.1 copy.87
  209.4 0.1 copy.88
  209.5 0.4 convolution_bitcast_fusion.1
  209.9 31.4 %all-to-all-done.3 = bf16[128,2,1024]{2,1,0:T(2,128)(2,1)S(1)} async-done(((bf16[128,2,1024]{2,1,0:T(2,128)(2,1)}), bf16[128,2,1024]{2,1,0:T(2,128)(2,1)S(1)}, u32[]{:S(2)}, u32[]{:S(2)}) %all-to-all-start.3) | async-done | bytes 524320 | tf_op jit(solution)/shard_map/all_to_all | solution.py:68
  241.3 0.4 fusion.49
  241.7 0.1 copy.81
  241.9 0.2 copy.89
  242.1 0.7 fusion.59
  (9 shorter events, 0.2 us)
Async XLA Ops:
  6.5 4.6 %collective-permute-start = (bf16[12,4096]{1,0:T(8,128)(2,1)}, bf16[12,4096]{1,0:T(8,128)(2,1)S(1)}, u32[]{:S(2)}, u32[]{:S(2)}) collective-permute-start(bf16[12,4096]{1,0:T(8,128)(2,1)} %param.7), channel_id=1, source_target_pairs={{0,128},{128,256},{256,384},{384,512},{512,640},{640,768},{768,896... | collective-permute-start | bytes 294920 | tf_op jit(solution)/shard_map/ppermute | solution.py:11
  14.1 60.3 %all-to-all-start = ((bf16[128,2,1024]{2,1,0:T(2,128)(2,1)}), bf16[128,2,1024]{2,1,0:T(2,128)(2,1)S(1)}, u32[]{:S(2)}, u32[]{:S(2)}) async-start(bf16[128,2,1024]{2,1,0:T(2,128)(2,1)} %bitcast.6), calls=%async_computation | async-start | bytes 1048576 | tf_op jit(solution)/shard_map/all_to_all | solution.py:53
  74.5 40.9 %all-to-all-start.2 = ((bf16[128,2,1024]{2,1,0:T(2,128)(2,1)}), bf16[128,2,1024]{2,1,0:T(2,128)(2,1)S(1)}, u32[]{:S(2)}, u32[]{:S(2)}) async-start(bf16[128,2,1024]{2,1,0:T(2,128)(2,1)} %bitcast.22), calls=%async_computation.3 | async-start | bytes 1048576 | tf_op jit(solution)/shard_map/all_to_all | solution.py:53
  80.5 42.8 %reduce-scatter.3.cloned.1.call-start = ((), (), s32[]{:S(2)}) async-start(), calls=%async_computation.6 | async-start | bytes 983040 | tf_op jit(solution)/shard_map/reduce_scatter | solution.py:61
  80.5 2.4 copy-start.1
  84.5 81.9 %reduce-scatter.5.cloned.1.call-start = ((), (), s32[]{:S(2)}) async-start(), calls=%async_computation.7 | async-start | bytes 983040 | tf_op jit(solution)/shard_map/reduce_scatter | solution.py:61
  115.3 2.4 copy-start.2
  118.3 21.1 %copy-start.3 = (bf16[2,768,1024]{2,1,0:T(8,128)(2,1)S(1)}, bf16[2,768,1024]{2,1,0:T(8,128)(2,1)}, u32[]{:S(2)}) copy-start(bf16[2,768,1024]{2,1,0:T(8,128)(2,1)} %param.13) | copy-start | bytes 9437188
  141.4 49.0 %all-to-all-start.1 = ((bf16[128,2,1024]{2,1,0:T(2,128)(2,1)}), bf16[128,2,1024]{2,1,0:T(2,128)(2,1)S(1)}, u32[]{:S(2)}, u32[]{:S(2)}) async-start(bf16[128,2,1024]{2,1,0:T(2,128)(2,1)} %copy.73), calls=%async_computation.2 | async-start | bytes 1048576 | tf_op jit(solution)/shard_map/all_to_all | solution.py:68
  167.3 41.6 %copy-start = (f32[12,8]{0,1:T(8,128)S(1)}, f32[12,8]{0,1:T(8,128)}, u32[]{:S(2)}) copy-start(f32[12,8]{0,1:T(8,128)} %param.10) | copy-start | bytes 1156
  190.4 50.9 %all-to-all-start.3 = ((bf16[128,2,1024]{2,1,0:T(2,128)(2,1)}), bf16[128,2,1024]{2,1,0:T(2,128)(2,1)S(1)}, u32[]{:S(2)}, u32[]{:S(2)}) async-start(bf16[128,2,1024]{2,1,0:T(2,128)(2,1)} %copy.79), calls=%async_computation.5 | async-start | bytes 1048576 | tf_op jit(solution)/shard_map/all_to_all | solution.py:68
Sparse Core Ops, SparseCore 0:
  84.7 38.4 reduce-scatter.2
  126.7 39.6 reduce-scatter.4

commit v8 on v2

--- a/solution.py
+++ b/solution.py
@@ -38,14 +38,13 @@
         tokens_here, expert_groups, slot_rows
     )
     normed_parts = normed.reshape(tokens_here, dp_groups, width_part)
+    devices = expert_groups * dp_groups
+    peer_rows = lax.all_to_all(normed_parts, "dp", split_axis=1, concat_axis=1, tiled=True)
+    peer_occupied = lax.all_gather(occupied, "dp", axis=0, tiled=False)
     send_rows = jnp.einsum(
-        "tes,tpw->epsw", occupied, normed_parts, preferred_element_type=jnp.float32
+        "qtes,tqw->eqsw", peer_occupied, peer_rows, preferred_element_type=jnp.float32
     ).astype(jnp.bfloat16)
-    devices = expert_groups * dp_groups
-    outgoing = send_rows.reshape(devices, slot_rows, width_part)
-    incoming = lax.all_to_all(
-        outgoing, ("expert", "dp"), split_axis=0, concat_axis=0, tiled=True
-    )
+    incoming = lax.all_to_all(send_rows, "expert", split_axis=0, concat_axis=0, tiled=True)
     grouped = incoming.reshape(devices, experts_here, CAP, width_part)
     gate_part = jnp.einsum("nxcd,xdf->nxcf", grouped, w_gate, preferred_element_type=jnp.float32)
     up_part = jnp.einsum("nxcd,xdf->nxcf", grouped, w_up, preferred_element_type=jnp.float32)

time: 225 us -> 242 us (1.076)
  blocking collectives: 136 us -> 141 us
  starting transfers between devices: 14.9 us -> 19.4 us
  local copies, waits for them, and re-layouts: 10.7 us -> 13.9 us
  matrix products: 5.65 us -> 8.1 us
    all_gather x0 -> x1, blocking collectives: none -> 13.8 us  [per_device(): peer_occupied = lax.all_gather(occupied, 'dp', axis=0, tiled=False)]
    all_to_all x1, blocking collectives: 80.9 us -> 71.2 us  [per_device(): lax.all_to_all(send_rows, 'expert', split_axis=0, concat_axis=0, tiled=True)]
    all_to_all x0 -> x1, starting transfers between devices: none -> 6.53 us  [per_device(): lax.all_to_all(normed_parts, 'dp', split_axis=1, concat_axis=1, tiled=True)]
    reshape x1, local copies, waits for them, and re-layouts: 0.12 us -> 3.3 us  [per_device(): grouped = incoming.reshape(devices, experts_here, CAP, width_part)]
  transfers between devices with their start and end apart: 2 -> 3, of which waited for: 2 -> 2; matrix products, arithmetic and copies ran while one was open for 1% -> 1% of each run, Pallas kernels for 0% -> 0%
where the time goes in v8:
time: 242 us; the launch traced here: 241 us
  blocking collectives  141 us (58%)
  waiting for transfers between devices  56.9 us (24%)
  starting transfers between devices  19.4 us (8%)
  local copies, waits for them, and re-layouts  13.9 us (6%)
  matrix products  8.1 us (3%)
    all_to_all x1, blocking collectives, per_device(): lax.all_to_all(send_rows, 'expert', split_axis=0, concat_axis=0, tiled=True)  71.2 us
    all_to_all x1, waiting for transfers between devices, per_device(): lax.all_to_all(returning, ('expert', 'dp'), split_axis=0, concat_axis=0,...  53.8 us
    all_to_all x1, blocking collectives, per_device(): lax.all_to_all(parts, 'dp', split_axis=0, concat_axis=0, tiled=False)  35.6 us
    all_gather x1, blocking collectives, per_device(): hidden = lax.all_gather(hidden_chunk, 'dp', axis=0, tiled=True)  20.1 us
    all_gather x1, blocking collectives, per_device(): peer_occupied = lax.all_gather(occupied, 'dp', axis=0, tiled=False)  13.8 us
    all_to_all x1, starting transfers between devices, per_device(): lax.all_to_all(returning, ('expert', 'dp'), split_axis=0, concat_axis=0,...  12.8 us
    all_to_all x1, starting transfers between devices, per_device(): lax.all_to_all(normed_parts, 'dp', split_axis=1, concat_axis=1, tiled=True)  6.53 us
  transfers between devices with their start and end apart: 3, of which 2 were waited for; matrix products, arithmetic and copies ran while one was open for 1% of the time, Pallas kernels for 0%

profile of v8, /device:TPU:26, one launch (start us, length us, event | category | flops | bytes accessed | tf_op | source)
XLA Modules:
  0.0 241.1 jit_solution(2932943965580561646)
XLA Ops:
  0.0 0.0 copy-start
  0.0 0.0 collective-permute-start
  0.0 0.9 copy.31
  0.9 0.1 eq.29
  1.0 0.1 fusion.28
  1.1 0.1 reduce_window_sum.11
  1.2 0.2 select_reduce_fusion.1
  1.4 0.1 reduce_sum.48
  1.5 3.1 %collective-permute-done = bf16[12,4096]{1,0:T(8,128)(2,1)S(1)} collective-permute-done((bf16[12,4096]{1,0:T(8,128)(2,1)}, bf16[12,4096]{1,0:T(8,128)(2,1)S(1)}, u32[]{:S(2)}, u32[]{:S(2)}) %collective-permute-start) | collective-permute-done | bytes 98336 | tf_op jit(solution)/shard_map/ppermute | solution.py:11
  4.6 0.1 fusion.22
  4.8 0.8 fusion.24
  5.6 0.1 reshape.66
  5.7 0.7 copy.35
  6.3 6.5 %all-to-all-start = ((bf16[12,4,1024]{2,0,1:T(8,128)(2,1)}), bf16[12,4,1024]{2,0,1:T(8,128)(2,1)S(1)}, u32[]{:S(2)}, u32[]{:S(2)}) async-start(bf16[12,4,1024]{2,0,1:T(8,128)(2,1)} %copy.35), calls=%async_computation | async-start | bytes 262144 | tf_op jit(solution)/shard_map/all_to_all | solution.py:42
  12.9 0.1 fusion.27
  13.0 0.1 copy.36
  13.1 0.1 copy.37
  13.2 13.8 %all_gather.6 = bf16[4,12,32,4]{2,3,1,0:T(4,128)(2,1)S(1)} all-gather(bf16[1,12,32,4]{2,3,1,0:T(4,128)(2,1)S(1)} %copy.37), channel_id=1, replica_groups=mesh['section'=8,'expert'=32,'dp'=4] {'dp'}, dimensions={0}, use_global_device_ids=true | all-gather | bytes 15360 | tf_op jit(solution)/shard_map/all_gather | solution.py:43
  27.0 0.0 all-to-all-done
  27.0 0.5 fusion.17
  27.5 0.8 copy.39
  28.3 71.2 %all_to_all.20 = bf16[32,4,4,1024]{3,2,1,0:T(4,128)(2,1)} all-to-all(bf16[32,4,4,1024]{3,2,1,0:T(4,128)(2,1)S(1)} %copy.39), channel_id=1, replica_groups=mesh['section'=8,'expert'=32,'dp'=4] {'expert'}, dimensions={0} | all-to-all | bytes 2097152 | tf_op jit(solution)/shard_map/all_to_all | solution.py:47
  99.5 3.3 %reshape.76 = bf16[128,2,2,1024]{3,2,1,0:T(2,128)(2,1)} reshape(bf16[32,4,4,1024]{3,2,1,0:T(4,128)(2,1)} %all_to_all.20) | data formatting | bytes 2097152 | tf_op jit(solution)/shard_map/reshape | solution.py:48
  102.8 0.0 copy-start.1
  102.8 0.0 copy-start.3
  102.8 3.4 %fusion.14 = bf16[2,128,2,768]{3,1,2,0:T(8,128)(2,1)S(1)} fusion(bf16[2,1024,768]{2,1,0:T(8,128)(2,1)} %param.12, bf16[128,2,2,1024]{3,2,1,0:T(2,128)(2,1)} %reshape.76), kind=kOutput, calls=%fused_computation.14 | convolution fusion | flops 805699584 | bytes 4980736 | tf_op jit(solution)/shard_map/nxcd,xdf->nxcf/dot_general | solution.py:50
  106.2 0.0 copy-done.1
  106.2 0.1 copy-done.3
  106.2 1.1 fusion.11
  107.3 0.1 pad_maximum_fusion
  107.5 0.1 copy.51
  107.6 35.6 %all_to_all.21 = bf16[4,2,32,2,2,768]{5,2,4,3,1,0:T(8,128)(2,1)S(1)} all-to-all(bf16[4,2,32,2,2,768]{5,2,4,3,1,0:T(8,128)(2,1)S(1)} %copy.51), channel_id=1, replica_groups=mesh['section'=8,'expert'=32,'dp'=4] {'dp'}, dimensions={0} | all-to-all | bytes 3145728 | tf_op jit(solution)/shard_map/all_to_all | solution.py:59
  143.2 0.2 convert_reduce_fusion
  143.4 0.1 fusion.21
  143.6 20.1 %all_gather.7 = bf16[128,2,2,768]{3,0,2,1:T(8,128)(2,1)S(1)} all-gather(bf16[32,2,2,768]{3,0,2,1:T(8,128)(2,1)S(1)} %fusion.21), channel_id=1, replica_groups=mesh['section'=8,'expert'=32,'dp'=4] {'dp'}, dimensions={0}, use_global_device_ids=true | all-gather | bytes 983040 | tf_op jit(solution)/shard_map/all_gather | solution.py:63
  163.7 0.0 copy-done
  163.7 1.0 fusion.8
  164.7 0.0 copy-start.2
  164.7 1.8 copy.43
  166.5 12.8 %all-to-all-start.3 = ((bf16[128,4,1024]{2,1,0:T(4,128)(2,1)}), bf16[128,4,1024]{2,1,0:T(4,128)(2,1)}, u32[]{:S(2)}, u32[]{:S(2)}) async-start(bf16[128,4,1024]{2,1,0:T(4,128)(2,1)} %copy.43), calls=%async_computation.3 | async-start | bytes 2097152 | tf_op jit(solution)/shard_map/all_to_all | solution.py:69
  179.3 0.0 copy-done.2
  179.4 0.1 copy.33
  179.5 0.1 select_reduce_fusion
  179.6 0.1 copy.34
  179.7 53.8 %all-to-all-done.3 = bf16[128,4,1024]{2,1,0:T(4,128)(2,1)} async-done(((bf16[128,4,1024]{2,1,0:T(4,128)(2,1)}), bf16[128,4,1024]{2,1,0:T(4,128)(2,1)}, u32[]{:S(2)}, u32[]{:S(2)}) %all-to-all-start.3) | async-done | bytes 1048608 | tf_op jit(solution)/shard_map/all_to_all | solution.py:69
  233.5 2.8 %copy.61 = bf16[32,4,4,1024]{3,1,0,2:T(4,128)(2,1)} copy(bf16[32,4,4,1024]{3,2,1,0:T(4,128)(2,1)} %bitcast.19) | data formatting | bytes 2097152 | tf_op jit(solution)/shard_map/reshape | solution.py:72
  236.3 2.6 %dot_general.24 = bf16[4096,32,4]{0,1,2:T(8,128)(2,1)} reshape(bf16[4,1024,32,4]{1,0,2,3:T(4,128)(2,1)} %bitcast.64) | data formatting | bytes 2097152 | tf_op jit(solution)/shard_map/tes,epsw->tpw/dot_general | solution.py:77
  238.9 2.2 fusion.1
  (5 shorter events, 0.0 us)
Async XLA Ops:
  0.0 163.7 %copy-start = (bf16[2,768,1024]{2,1,0:T(8,128)(2,1)S(1)}, bf16[2,768,1024]{2,1,0:T(8,128)(2,1)}, u32[]{:S(2)}) copy-start(bf16[2,768,1024]{2,1,0:T(8,128)(2,1)} %param.13) | copy-start | bytes 9437188
  0.0 4.6 %collective-permute-start = (bf16[12,4096]{1,0:T(8,128)(2,1)}, bf16[12,4096]{1,0:T(8,128)(2,1)S(1)}, u32[]{:S(2)}, u32[]{:S(2)}) collective-permute-start(bf16[12,4096]{1,0:T(8,128)(2,1)} %param.7), channel_id=1, source_target_pairs={{0,128},{128,256},{256,384},{384,512},{512,640},{640,768},{768,896... | collective-permute-start | bytes 294920 | tf_op jit(solution)/shard_map/ppermute | solution.py:11
  6.3 20.7 %all-to-all-start = ((bf16[12,4,1024]{2,0,1:T(8,128)(2,1)}), bf16[12,4,1024]{2,0,1:T(8,128)(2,1)S(1)}, u32[]{:S(2)}, u32[]{:S(2)}) async-start(bf16[12,4,1024]{2,0,1:T(8,128)(2,1)} %copy.35), calls=%async_computation | async-start | bytes 262144 | tf_op jit(solution)/shard_map/all_to_all | solution.py:42
  102.8 3.4 %copy-start.1 = (bf16[128,2,2,1024]{3,2,1,0:T(2,128)(2,1)S(1)}, bf16[128,2,2,1024]{3,2,1,0:T(2,128)(2,1)}, u32[]{:S(2)}) copy-start(bf16[128,2,2,1024]{3,2,1,0:T(2,128)(2,1)} %reshape.76) | copy-start | bytes 3145732
  102.8 3.5 %copy-start.3 = (bf16[2,1024,768]{2,1,0:T(8,128)(2,1)S(1)}, bf16[2,1024,768]{2,1,0:T(8,128)(2,1)}, u32[]{:S(2)}) copy-start(bf16[2,1024,768]{2,1,0:T(8,128)(2,1)} %param.11) | copy-start | bytes 9437188
  164.7 14.7 %copy-start.2 = (f32[12,8]{0,1:T(8,128)S(1)}, f32[12,8]{0,1:T(8,128)}, u32[]{:S(2)}) copy-start(f32[12,8]{0,1:T(8,128)} %param.10) | copy-start | bytes 1156
  166.5 67.0 %all-to-all-start.3 = ((bf16[128,4,1024]{2,1,0:T(4,128)(2,1)}), bf16[128,4,1024]{2,1,0:T(4,128)(2,1)}, u32[]{:S(2)}, u32[]{:S(2)}) async-start(bf16[128,4,1024]{2,1,0:T(4,128)(2,1)} %copy.43), calls=%async_computation.3 | async-start | bytes 2097152 | tf_op jit(solution)/shard_map/all_to_all | solution.py:69

commit v9 on v2

--- a/solution.py
+++ b/solution.py
@@ -61,7 +61,8 @@
     summed = jnp.sum(parts.astype(jnp.float32), axis=0)
     gate_full, up_full = summed[0], summed[1]
     hidden_chunk = (jax.nn.silu(gate_full) * up_full).astype(jnp.bfloat16)
-    hidden = lax.all_gather(hidden_chunk, "dp", axis=0, tiled=True)
+    copies = jnp.broadcast_to(hidden_chunk[None], (dp_groups,) + hidden_chunk.shape)
+    hidden = lax.all_to_all(copies, "dp", split_axis=0, concat_axis=0, tiled=False)
     hidden = hidden.reshape(devices, experts_here, CAP, -1)
     expert_out = jnp.einsum(
         "nxcf,xfd->nxcd", hidden, w_down, preferred_element_type=jnp.float32

time: 225 us -> 229 us (1.018)
  blocking collectives: 136 us -> 141 us
  starting transfers between devices: 14.9 us -> 12.3 us
    all_to_all x0 -> x1, blocking collectives: none -> 24.8 us  [per_device(): lax.all_to_all(copies, 'dp', split_axis=0, concat_axis=0, tiled=False)]
    all_gather x1 -> x0, blocking collectives: 19.8 us -> none  [per_device(): hidden = lax.all_gather(hidden_chunk, 'dp', axis=0, tiled=True)]
    all_to_all x1, starting transfers between devices: 14.9 us -> 12.3 us  [per_device(): lax.all_to_all(returning, ('expert', 'dp'), split_axis=0, concat_axis=0,...]
where the time goes in v9:
time: 229 us
  blocking collectives  141 us (62%)
  waiting for transfers between devices  56.7 us (25%)
  starting transfers between devices  12.3 us (5%)
  local copies, waits for them, and re-layouts  10.8 us (5%)
  matrix products  5.64 us (2%)
    all_to_all x1, blocking collectives, per_device(): lax.all_to_all(outgoing, ('expert', 'dp'), split_axis=0, concat_axis=0, t...  80.9 us
    all_to_all x1, waiting for transfers between devices, per_device(): lax.all_to_all(returning, ('expert', 'dp'), split_axis=0, concat_axis=0,...  53.9 us
    all_to_all x1, blocking collectives, per_device(): lax.all_to_all(parts, 'dp', split_axis=0, concat_axis=0, tiled=False)  35.3 us
    all_to_all x1, blocking collectives, per_device(): lax.all_to_all(copies, 'dp', split_axis=0, concat_axis=0, tiled=False)  24.8 us
    all_to_all x1, starting transfers between devices, per_device(): lax.all_to_all(returning, ('expert', 'dp'), split_axis=0, concat_axis=0,...  12.3 us
  transfers between devices with their start and end apart: 2, of which 2 were waited for; matrix products, arithmetic and copies ran while one was open for 1% of the time, Pallas kernels for 0%

profile of v9, /device:TPU:26, one launch (start us, length us, event | category | flops | bytes accessed | tf_op | source)
XLA Modules:
  0.0 228.8 jit_solution(14584788440984665034)
XLA Ops:
  0.0 0.0 copy-start
  0.0 0.0 collective-permute-start
  0.0 0.9 copy.33
  0.9 0.1 eq.29
  1.0 0.1 fusion.25
  1.1 0.1 reduce_window_sum.11
  1.2 0.2 select_reduce_fusion.1
  1.4 0.1 reduce_sum.48
  1.5 0.1 fusion.24
  1.6 0.1 copy.37
  1.8 0.1 copy.39
  1.9 2.7 %collective-permute-done = bf16[12,4096]{1,0:T(8,128)(2,1)S(1)} collective-permute-done((bf16[12,4096]{1,0:T(8,128)(2,1)}, bf16[12,4096]{1,0:T(8,128)(2,1)S(1)}, u32[]{:S(2)}, u32[]{:S(2)}) %collective-permute-start) | collective-permute-done | bytes 98336 | tf_op jit(solution)/shard_map/ppermute | solution.py:11
  4.6 0.1 fusion.19
  4.8 0.8 fusion.21
  5.6 0.1 reshape.63
  5.7 0.5 fusion.17
  6.2 0.0 copy-start.2
  6.2 0.8 copy.40
  7.0 80.9 %all_to_all.20 = bf16[128,4,1024]{2,1,0:T(4,128)(2,1)S(1)} all-to-all(bf16[128,4,1024]{2,1,0:T(4,128)(2,1)S(1)} %bitcast.60), channel_id=1, replica_groups=mesh['section'=8,'expert'=32,'dp'=4] {'expert','dp'}, dimensions={0} | all-to-all | bytes 2097152 | tf_op jit(solution)/shard_map/all_to_all | solution.py:46
  87.9 0.0 copy-start.3
  87.9 0.3 copy.41
  88.3 0.0 copy-done.2
  88.3 1.0 fusion.11
  89.3 0.6 copy-done.3
  89.8 1.0 fusion.14
  90.8 0.1 pad_maximum_fusion
  91.0 0.1 copy.54
  91.1 35.3 %all_to_all.21 = bf16[4,2,32,2,2,768]{5,2,4,3,1,0:T(8,128)(2,1)S(1)} all-to-all(bf16[4,2,32,2,2,768]{5,2,4,3,1,0:T(8,128)(2,1)S(1)} %copy.54), channel_id=1, replica_groups=mesh['section'=8,'expert'=32,'dp'=4] {'dp'}, dimensions={0} | all-to-all | bytes 3145728 | tf_op jit(solution)/shard_map/all_to_all | solution.py:60
  126.5 0.2 convert_reduce_fusion
  126.7 0.1 fusion.22
  126.8 0.1 broadcast_in_dim.30
  126.9 24.8 %all_to_all.22 = bf16[4,32,2,2,768]{4,1,3,2,0:T(8,128)(2,1)S(1)} all-to-all(bf16[4,32,2,2,768]{4,1,3,2,0:T(8,128)(2,1)S(1)} %broadcast_in_dim.30), channel_id=1, replica_groups=mesh['section'=8,'expert'=32,'dp'=4] {'dp'}, dimensions={0} | all-to-all | bytes 1572864 | tf_op jit(solution)/shard_map/all_to_all | solution.py:65
  151.7 0.1 copy.44
  151.7 0.0 copy-done
  151.7 1.0 fusion.8
  152.7 0.0 copy-start.1
  152.8 1.8 copy.45
  154.6 12.3 %all-to-all-start.3 = ((bf16[128,4,1024]{2,1,0:T(4,128)(2,1)}), bf16[128,4,1024]{2,1,0:T(4,128)(2,1)}, u32[]{:S(2)}, u32[]{:S(2)}) async-start(bf16[128,4,1024]{2,1,0:T(4,128)(2,1)} %copy.45), calls=%async_computation.3 | async-start | bytes 2097152 | tf_op jit(solution)/shard_map/all_to_all | solution.py:71
  166.9 0.0 copy-done.1
  166.9 0.1 copy.35
  167.0 0.1 select_reduce_fusion
  167.1 0.1 copy.36
  167.3 53.9 %all-to-all-done.3 = bf16[128,4,1024]{2,1,0:T(4,128)(2,1)} async-done(((bf16[128,4,1024]{2,1,0:T(4,128)(2,1)}), bf16[128,4,1024]{2,1,0:T(4,128)(2,1)}, u32[]{:S(2)}, u32[]{:S(2)}) %all-to-all-start.3) | async-done | bytes 1048608 | tf_op jit(solution)/shard_map/all_to_all | solution.py:71
  221.2 2.8 %copy.60 = bf16[32,4,4,1024]{3,1,0,2:T(4,128)(2,1)} copy(bf16[32,4,4,1024]{3,2,1,0:T(4,128)(2,1)} %bitcast.21) | data formatting | bytes 2097152 | tf_op jit(solution)/shard_map/reshape | solution.py:74
  224.0 2.6 %dot_general.24 = bf16[4096,32,4]{0,1,2:T(8,128)(2,1)} reshape(bf16[4,1024,32,4]{1,0,2,3:T(4,128)(2,1)} %bitcast.61) | data formatting | bytes 2097152 | tf_op jit(solution)/shard_map/tes,epsw->tpw/dot_general | solution.py:79
  226.6 2.2 fusion.1
  (4 shorter events, 0.0 us)
Async XLA Ops:
  0.0 151.7 %copy-start = (bf16[2,768,1024]{2,1,0:T(8,128)(2,1)S(1)}, bf16[2,768,1024]{2,1,0:T(8,128)(2,1)}, u32[]{:S(2)}) copy-start(bf16[2,768,1024]{2,1,0:T(8,128)(2,1)} %param.13) | copy-start | bytes 9437188
  0.0 4.6 %collective-permute-start = (bf16[12,4096]{1,0:T(8,128)(2,1)}, bf16[12,4096]{1,0:T(8,128)(2,1)S(1)}, u32[]{:S(2)}, u32[]{:S(2)}) collective-permute-start(bf16[12,4096]{1,0:T(8,128)(2,1)} %param.7), channel_id=1, source_target_pairs={{0,128},{128,256},{256,384},{384,512},{512,640},{640,768},{768,896... | collective-permute-start | bytes 294920 | tf_op jit(solution)/shard_map/ppermute | solution.py:11
  6.2 82.1 %copy-start.2 = (bf16[2,1024,768]{2,1,0:T(8,128)(2,1)S(1)}, bf16[2,1024,768]{2,1,0:T(8,128)(2,1)}, u32[]{:S(2)}) copy-start(bf16[2,1024,768]{2,1,0:T(8,128)(2,1)} %param.11) | copy-start | bytes 9437188
  87.9 1.9 copy-start.3
  152.7 14.2 %copy-start.1 = (f32[12,8]{0,1:T(8,128)S(1)}, f32[12,8]{0,1:T(8,128)}, u32[]{:S(2)}) copy-start(f32[12,8]{0,1:T(8,128)} %param.10) | copy-start | bytes 1156
  154.6 66.6 %all-to-all-start.3 = ((bf16[128,4,1024]{2,1,0:T(4,128)(2,1)}), bf16[128,4,1024]{2,1,0:T(4,128)(2,1)}, u32[]{:S(2)}, u32[]{:S(2)}) async-start(bf16[128,4,1024]{2,1,0:T(4,128)(2,1)} %copy.45), calls=%async_computation.3 | async-start | bytes 2097152 | tf_op jit(solution)/shard_map/all_to_all | solution.py:71

commit v10 on v2

--- a/solution.py
+++ b/solution.py
@@ -12,10 +12,11 @@
 
 
 def per_device(panel, norm_gain, expert_ids, gate_scores, w_gate, w_up, w_down):
-    arrived = passed_along(panel, "section", 1)
+    panel_f = panel.astype(jnp.float32)
+    mean_sq = jnp.mean(panel_f * panel_f, axis=-1, keepdims=True)
+    normed_here = (panel_f * lax.rsqrt(mean_sq + 1e-06) * norm_gain).astype(jnp.bfloat16)
+    arrived, normed = passed_along(jnp.stack([panel, normed_here]), "section", 1)
     arrived_f = arrived.astype(jnp.float32)
-    mean_sq = jnp.mean(arrived_f * arrived_f, axis=-1, keepdims=True)
-    normed = (arrived_f * lax.rsqrt(mean_sq + 1e-06) * norm_gain).astype(jnp.bfloat16)
     experts_here = w_gate.shape[0]
     width_part = w_gate.shape[1]
     expert_groups = lax.axis_size("expert")

time: 225 us -> 229 us (1.018)
  no operation moved by 1% of the time
where the time goes in v10:
time: 229 us
  blocking collectives  136 us (59%)
  waiting for transfers between devices  57 us (25%)
  starting transfers between devices  14.6 us (6%)
  local copies, waits for them, and re-layouts  11.5 us (5%)
  matrix products  5.64 us (2%)
  other arithmetic  4.32 us (2%)
    all_to_all x1, blocking collectives, per_device(): lax.all_to_all(outgoing, ('expert', 'dp'), split_axis=0, concat_axis=0, t...  80.7 us
    all_to_all x1, waiting for transfers between devices, per_device(): lax.all_to_all(returning, ('expert', 'dp'), split_axis=0, concat_axis=0,...  52.9 us
    all_to_all x1, blocking collectives, per_device(): lax.all_to_all(parts, 'dp', split_axis=0, concat_axis=0, tiled=False)  35.2 us
    all_gather x1, blocking collectives, per_device(): hidden = lax.all_gather(hidden_chunk, 'dp', axis=0, tiled=True)  19.7 us
    all_to_all x1, starting transfers between devices, per_device(): lax.all_to_all(returning, ('expert', 'dp'), split_axis=0, concat_axis=0,...  14.6 us
  transfers between devices with their start and end apart: 2, of which 2 were waited for; matrix products, arithmetic and copies ran while one was open for 1% of the time, Pallas kernels for 0%

profile of v10, /device:TPU:26, one launch (start us, length us, event | category | flops | bytes accessed | tf_op | source)
XLA Modules:
  0.0 228.8 jit_solution(11543968348404977408)
XLA Ops:
  0.0 0.0 copy-start
  0.0 1.2 fusion.18
  1.2 1.0 fusion.22
  2.2 0.9 pad_maximum_fusion.1
  3.2 0.0 collective-permute-start
  3.2 0.8 copy.31
  4.0 0.1 eq.29
  4.1 0.1 fusion.25
  4.2 0.1 reduce_window_sum.11
  4.3 0.2 select_reduce_fusion.1
  4.5 0.1 reduce_sum.49
  4.6 0.1 fusion.24
  4.7 0.1 copy.35
  4.8 0.1 copy.37
  4.9 4.2 %collective-permute-done = bf16[2,12,4096]{2,1,0:T(8,128)(2,1)} collective-permute-done((bf16[2,12,4096]{2,1,0:T(8,128)(2,1)S(1)}, bf16[2,12,4096]{2,1,0:T(8,128)(2,1)}, u32[]{:S(2)}, u32[]{:S(2)}) %collective-permute-start) | collective-permute-done | bytes 196640 | tf_op jit(solution)/shard_map/ppermute | solution.py:11
  9.1 0.9 unstack.10
  10.0 0.1 reshape_unstack.3
  10.1 0.5 fusion.15
  10.6 0.0 copy-start.2
  10.6 0.8 copy.38
  11.4 80.7 %all_to_all.15 = bf16[128,4,1024]{2,1,0:T(4,128)(2,1)S(1)} all-to-all(bf16[128,4,1024]{2,1,0:T(4,128)(2,1)S(1)} %bitcast.73), channel_id=1, replica_groups=mesh['section'=8,'expert'=32,'dp'=4] {'expert','dp'}, dimensions={0} | all-to-all | bytes 2097152 | tf_op jit(solution)/shard_map/all_to_all | solution.py:47
  92.2 0.0 copy-start.3
  92.2 0.3 copy.39
  92.5 0.0 copy-done.2
  92.5 1.0 fusion.9
  93.5 0.6 copy-done.3
  94.0 1.0 fusion.12
  95.0 0.1 pad_maximum_fusion
  95.2 0.1 copy.51
  95.3 35.2 %all_to_all.16 = bf16[4,2,32,2,2,768]{5,2,4,3,1,0:T(8,128)(2,1)S(1)} all-to-all(bf16[4,2,32,2,2,768]{5,2,4,3,1,0:T(8,128)(2,1)S(1)} %copy.51), channel_id=1, replica_groups=mesh['section'=8,'expert'=32,'dp'=4] {'dp'}, dimensions={0} | all-to-all | bytes 3145728 | tf_op jit(solution)/shard_map/all_to_all | solution.py:61
  130.6 0.2 convert_reduce_fusion
  130.8 0.1 fusion.17
  130.9 19.7 %all_gather.3 = bf16[128,2,2,768]{3,0,2,1:T(8,128)(2,1)S(1)} all-gather(bf16[32,2,2,768]{3,0,2,1:T(8,128)(2,1)S(1)} %fusion.17), channel_id=1, replica_groups=mesh['section'=8,'expert'=32,'dp'=4] {'dp'}, dimensions={0}, use_global_device_ids=true | all-gather | bytes 983040 | tf_op jit(solution)/shard_map/all_gather | solution.py:65
  150.6 0.0 copy-done
  150.6 1.0 fusion.6
  151.6 0.0 copy-start.1
  151.6 1.8 copy.42
  153.4 14.6 %all-to-all-start.2 = ((bf16[128,4,1024]{2,1,0:T(4,128)(2,1)}), bf16[128,4,1024]{2,1,0:T(4,128)(2,1)}, u32[]{:S(2)}, u32[]{:S(2)}) async-start(bf16[128,4,1024]{2,1,0:T(4,128)(2,1)} %copy.42), calls=%async_computation.2 | async-start | bytes 2097152 | tf_op jit(solution)/shard_map/all_to_all | solution.py:71
  168.0 0.0 copy-done.1
  168.1 0.1 copy.33
  168.2 0.1 select_reduce_fusion
  168.3 0.1 copy.34
  168.4 52.9 %all-to-all-done.2 = bf16[128,4,1024]{2,1,0:T(4,128)(2,1)} async-done(((bf16[128,4,1024]{2,1,0:T(4,128)(2,1)}), bf16[128,4,1024]{2,1,0:T(4,128)(2,1)}, u32[]{:S(2)}, u32[]{:S(2)}) %all-to-all-start.2) | async-done | bytes 1048608 | tf_op jit(solution)/shard_map/all_to_all | solution.py:71
  221.3 2.8 %copy.59 = bf16[32,4,4,1024]{3,1,0,2:T(4,128)(2,1)} copy(bf16[32,4,4,1024]{3,2,1,0:T(4,128)(2,1)} %bitcast.24) | data formatting | bytes 2097152 | tf_op jit(solution)/shard_map/reshape | solution.py:74
  224.1 2.6 %dot_general.24 = bf16[4096,32,4]{0,1,2:T(8,128)(2,1)} reshape(bf16[4,1024,32,4]{1,0,2,3:T(4,128)(2,1)} %bitcast.74) | data formatting | bytes 2097152 | tf_op jit(solution)/shard_map/tes,epsw->tpw/dot_general | solution.py:79
  226.7 2.2 fusion.21
  (4 shorter events, 0.0 us)
Async XLA Ops:
  0.0 150.6 %copy-start = (bf16[2,768,1024]{2,1,0:T(8,128)(2,1)S(1)}, bf16[2,768,1024]{2,1,0:T(8,128)(2,1)}, u32[]{:S(2)}) copy-start(bf16[2,768,1024]{2,1,0:T(8,128)(2,1)} %param.13) | copy-start | bytes 9437188
  3.2 5.9 %collective-permute-start = (bf16[2,12,4096]{2,1,0:T(8,128)(2,1)S(1)}, bf16[2,12,4096]{2,1,0:T(8,128)(2,1)}, u32[]{:S(2)}, u32[]{:S(2)}) collective-permute-start(bf16[2,12,4096]{2,1,0:T(8,128)(2,1)S(1)} %pad_maximum_fusion.1), channel_id=1, source_target_pairs={{0,128},{128,256},{256,384},{384,512},{512,640},{640,768},{768,896... | collective-permute-start | bytes 589832 | tf_op jit(solution)/shard_map/ppermute | solution.py:11
  10.6 81.9 %copy-start.2 = (bf16[2,1024,768]{2,1,0:T(8,128)(2,1)S(1)}, bf16[2,1024,768]{2,1,0:T(8,128)(2,1)}, u32[]{:S(2)}) copy-start(bf16[2,1024,768]{2,1,0:T(8,128)(2,1)} %param.11) | copy-start | bytes 9437188
  92.2 1.9 copy-start.3
  151.6 16.4 %copy-start.1 = (f32[12,8]{0,1:T(8,128)S(1)}, f32[12,8]{0,1:T(8,128)}, u32[]{:S(2)}) copy-start(f32[12,8]{0,1:T(8,128)} %param.10) | copy-start | bytes 1156
  153.4 67.8 %all-to-all-start.2 = ((bf16[128,4,1024]{2,1,0:T(4,128)(2,1)}), bf16[128,4,1024]{2,1,0:T(4,128)(2,1)}, u32[]{:S(2)}, u32[]{:S(2)}) async-start(bf16[128,4,1024]{2,1,0:T(4,128)(2,1)} %copy.42), calls=%async_computation.2 | async-start | bytes 2097152 | tf_op jit(solution)/shard_map/all_to_all | solution.py:71

commit v11 on v1

--- a/solution.py
+++ b/solution.py
@@ -49,11 +49,23 @@
     grouped = incoming.reshape(devices, experts_here, CAP, width_part)
     gate_part = jnp.einsum("nxcd,xdf->nxcf", grouped, w_gate, preferred_element_type=jnp.float32)
     up_part = jnp.einsum("nxcd,xdf->nxcf", grouped, w_up, preferred_element_type=jnp.float32)
+    chunks = gate_part.shape[0] // dp_groups
     gate_full, up_full = (
-        lax.psum(gate_part.astype(jnp.bfloat16), "dp").astype(jnp.float32),
-        lax.psum(up_part.astype(jnp.bfloat16), "dp").astype(jnp.float32),
+        jnp.sum(
+            lax.all_to_all(
+                part.reshape(dp_groups, chunks, experts_here, CAP, -1).astype(jnp.bfloat16),
+                "dp",
+                split_axis=0,
+                concat_axis=0,
+                tiled=False,
+            ).astype(jnp.float32),
+            axis=0,
+        )
+        for part in (gate_part, up_part)
     )
-    hidden = (jax.nn.silu(gate_full) * up_full).astype(jnp.bfloat16)
+    hidden_chunk = (jax.nn.silu(gate_full) * up_full).astype(jnp.bfloat16)
+    hidden = lax.all_gather(hidden_chunk, "dp", axis=0, tiled=True)
+    hidden = hidden.reshape(devices, experts_here, CAP, -1)
     expert_out = jnp.einsum(
         "nxcf,xfd->nxcd", hidden, w_down, preferred_element_type=jnp.float32
     ).astype(jnp.bfloat16)

time: 279 us -> 232 us (0.83)
  the two profiles are of different devices: /device:TPU:26 before, /device:TPU:28 now
where the time goes in v11:
time: 232 us; the launch traced here: 231 us
  blocking collectives  98.1 us (42%)
  waiting for transfers between devices  82.7 us (36%)
  starting transfers between devices  25.1 us (11%)
  local copies, waits for them, and re-layouts  12.9 us (6%)
  matrix products  7.84 us (3%)
  other arithmetic  4.31 us (2%)
    all_to_all x1, blocking collectives, per_device(): lax.all_to_all(outgoing, ('expert', 'dp'), split_axis=0, concat_axis=0, t...  80.7 us
    all_to_all x1, waiting for transfers between devices, per_device(): lax.all_to_all(returning, ('expert', 'dp'), split_axis=0, concat_axis=0,...  49.6 us
    all_to_all x2, waiting for transfers between devices, per_device(): lax.all_to_all(part.reshape(dp_groups, chunks, experts_here, CAP, -1).ast...  30.5 us
    all_gather x1, blocking collectives, per_device(): hidden = lax.all_gather(hidden_chunk, 'dp', axis=0, tiled=True)  17.4 us
    all_to_all x1, starting transfers between devices, per_device(): lax.all_to_all(returning, ('expert', 'dp'), split_axis=0, concat_axis=0,...  15.4 us
    all_to_all x2, starting transfers between devices, per_device(): lax.all_to_all(part.reshape(dp_groups, chunks, experts_here, CAP, -1).ast...  9.73 us
  transfers between devices with their start and end apart: 4, of which 4 were waited for; matrix products, arithmetic and copies ran while one was open for 3% of the time, Pallas kernels for 0%

profile of v11, /device:TPU:28, one launch (start us, length us, event | category | flops | bytes accessed | tf_op | source)
XLA Modules:
  0.0 231.2 jit_solution(4973284290106442302)
XLA Ops:
  0.0 0.0 copy-start
  0.0 0.0 collective-permute-start
  0.0 0.9 copy.32
  0.9 0.1 eq.29
  1.0 0.1 fusion.23
  1.1 0.1 reduce_window_sum.11
  1.2 0.2 select_reduce_fusion.1
  1.4 0.1 reduce_sum.57
  1.5 0.1 fusion.22
  1.6 0.1 copy.36
  1.8 0.1 copy.38
  1.9 2.7 %collective-permute-done = bf16[12,4096]{1,0:T(8,128)(2,1)S(1)} collective-permute-done((bf16[12,4096]{1,0:T(8,128)(2,1)}, bf16[12,4096]{1,0:T(8,128)(2,1)S(1)}, u32[]{:S(2)}, u32[]{:S(2)}) %collective-permute-start) | collective-permute-done | bytes 98336 | tf_op jit(solution)/shard_map/ppermute | solution.py:11
  4.6 0.0 copy-start.1
  4.6 0.1 fusion.18
  4.8 0.8 fusion.20
  5.6 0.1 reshape.64
  5.7 0.5 fusion.17
  6.2 0.0 copy-start.5
  6.2 0.8 copy.39
  7.0 80.7 %all_to_all.20 = bf16[128,4,1024]{2,1,0:T(4,128)(2,1)S(1)} all-to-all(bf16[128,4,1024]{2,1,0:T(4,128)(2,1)S(1)} %bitcast.57), channel_id=1, replica_groups=mesh['section'=8,'expert'=32,'dp'=4] {'expert','dp'}, dimensions={0} | all-to-all | bytes 2097152 | tf_op jit(solution)/shard_map/all_to_all | solution.py:46
  87.7 0.3 copy.40
  88.0 0.0 copy-done.1
  88.1 0.0 copy-start.3
  88.1 1.0 copy-done.3
  89.0 0.0 copy-done.5
  89.0 1.0 fusion.14
  90.0 0.9 copy.42
  91.0 4.4 %all-to-all-start.2 = ((bf16[4,32,2,2,768]{4,1,3,2,0:T(8,128)(2,1)}), bf16[4,32,2,2,768]{4,1,3,2,0:T(8,128)(2,1)}, u32[]{:S(2)}, u32[]{:S(2)}) async-start(bf16[4,32,2,2,768]{4,1,3,2,0:T(8,128)(2,1)} %copy.42), calls=%async_computation.2 | async-start | bytes 1572864 | tf_op jit(solution)/shard_map/all_to_all | solution.py:55
  95.4 3.2 %fusion.11 = bf16[2,128,2,768]{3,1,2,0:T(8,128)(2,1)S(1)} fusion(bf16[128,2,2,1024]{3,0,2,1:T(8,128)(2,1)} %bitcast.60, bf16[2,1024,768]{2,1,0:T(8,128)(2,1)} %param.11), kind=kOutput, calls=%fused_computation.13 | convolution fusion | flops 805699584 | bytes 4980736 | tf_op jit(solution)/shard_map/nxcd,xdf->nxcf/dot_general | solution.py:50
  98.6 0.9 copy.41
  99.5 11.8 %all-to-all-done.2 = bf16[4,32,2,2,768]{4,1,3,2,0:T(8,128)(2,1)} async-done(((bf16[4,32,2,2,768]{4,1,3,2,0:T(8,128)(2,1)}), bf16[4,32,2,2,768]{4,1,3,2,0:T(8,128)(2,1)}, u32[]{:S(2)}, u32[]{:S(2)}) %all-to-all-start.2) | async-done | bytes 786464 | tf_op jit(solution)/shard_map/all_to_all | solution.py:55
  111.3 5.4 %all-to-all-start.1 = ((bf16[4,32,2,2,768]{4,1,3,2,0:T(8,128)(2,1)}), bf16[4,32,2,2,768]{4,1,3,2,0:T(8,128)(2,1)}, u32[]{:S(2)}, u32[]{:S(2)}) async-start(bf16[4,32,2,2,768]{4,1,3,2,0:T(8,128)(2,1)} %copy.41), calls=%async_computation.1 | async-start | bytes 1572864 | tf_op jit(solution)/shard_map/all_to_all | solution.py:55
  116.7 1.3 convert_reduce_fusion
  117.9 18.6 %all-to-all-done.1 = bf16[4,32,2,2,768]{4,1,3,2,0:T(8,128)(2,1)} async-done(((bf16[4,32,2,2,768]{4,1,3,2,0:T(8,128)(2,1)}), bf16[4,32,2,2,768]{4,1,3,2,0:T(8,128)(2,1)}, u32[]{:S(2)}, u32[]{:S(2)}) %all-to-all-start.1) | async-done | bytes 786464 | tf_op jit(solution)/shard_map/all_to_all | solution.py:55
  136.6 1.3 convert_reduce_fusion.1
  137.9 0.1 multiply_convert_fusion
  138.0 17.4 %all_gather.3 = bf16[128,2,2,768]{3,0,2,1:T(8,128)(2,1)S(1)} all-gather(bf16[32,2,2,768]{3,0,2,1:T(8,128)(2,1)S(1)} %multiply_convert_fusion), channel_id=1, replica_groups=mesh['section'=8,'expert'=32,'dp'=4] {'dp'}, dimensions={0}, use_global_device_ids=true | all-gather | bytes 983040 | tf_op jit(solution)/shard_map/all_gather | solution.py:67
  155.4 0.0 copy-done
  155.4 1.0 fusion.8
  156.4 0.0 copy-start.4
  156.4 1.8 copy.43
  158.2 0.0 copy-start.2
  158.2 15.4 %all-to-all-start.3 = ((bf16[128,4,1024]{2,1,0:T(4,128)(2,1)}), bf16[128,4,1024]{2,1,0:T(4,128)(2,1)}, u32[]{:S(2)}, u32[]{:S(2)}) async-start(bf16[128,4,1024]{2,1,0:T(4,128)(2,1)} %copy.43), calls=%async_computation.3 | async-start | bytes 2097152 | tf_op jit(solution)/shard_map/all_to_all | solution.py:73
  173.6 0.0 copy-done.4
  173.7 0.1 copy.34
  173.8 0.1 select_reduce_fusion
  173.9 0.1 copy.35
  174.0 49.6 %all-to-all-done.3 = bf16[128,4,1024]{2,1,0:T(4,128)(2,1)} async-done(((bf16[128,4,1024]{2,1,0:T(4,128)(2,1)}), bf16[128,4,1024]{2,1,0:T(4,128)(2,1)}, u32[]{:S(2)}, u32[]{:S(2)}) %all-to-all-start.3) | async-done | bytes 1048608 | tf_op jit(solution)/shard_map/all_to_all | solution.py:73
  223.6 2.8 %copy.57 = bf16[32,4,4,1024]{3,1,0,2:T(4,128)(2,1)} copy(bf16[32,4,4,1024]{3,2,1,0:T(4,128)(2,1)} %bitcast.19) | data formatting | bytes 2097152 | tf_op jit(solution)/shard_map/reshape | solution.py:76
  226.4 2.6 %dot_general.24 = bf16[4096,32,4]{0,1,2:T(8,128)(2,1)} reshape(bf16[4,1024,32,4]{1,0,2,3:T(4,128)(2,1)} %bitcast.58) | data formatting | bytes 2097152 | tf_op jit(solution)/shard_map/tes,epsw->tpw/dot_general | solution.py:81
  229.0 0.0 copy-done.2
  229.0 2.2 fusion.1
  (4 shorter events, 0.0 us)
Async XLA Ops:
  0.0 155.4 %copy-start = (bf16[2,768,1024]{2,1,0:T(8,128)(2,1)S(1)}, bf16[2,768,1024]{2,1,0:T(8,128)(2,1)}, u32[]{:S(2)}) copy-start(bf16[2,768,1024]{2,1,0:T(8,128)(2,1)} %param.13) | copy-start | bytes 9437188
  0.0 4.6 %collective-permute-start = (bf16[12,4096]{1,0:T(8,128)(2,1)}, bf16[12,4096]{1,0:T(8,128)(2,1)S(1)}, u32[]{:S(2)}, u32[]{:S(2)}) collective-permute-start(bf16[12,4096]{1,0:T(8,128)(2,1)} %param.7), channel_id=1, source_target_pairs={{0,128},{128,256},{256,384},{384,512},{512,640},{640,768},{768,896... | collective-permute-start | bytes 294920 | tf_op jit(solution)/shard_map/ppermute | solution.py:11
  4.6 83.4 %copy-start.1 = (bf16[12,4096]{1,0:T(8,128)(2,1)}, bf16[12,4096]{1,0:T(8,128)(2,1)S(1)}, u32[]{:S(2)}) copy-start(bf16[12,4096]{1,0:T(8,128)(2,1)S(1)} %collective-permute-done) | copy-start | bytes 294916
  6.2 82.9 %copy-start.5 = (bf16[2,1024,768]{2,1,0:T(8,128)(2,1)S(1)}, bf16[2,1024,768]{2,1,0:T(8,128)(2,1)}, u32[]{:S(2)}) copy-start(bf16[2,1024,768]{2,1,0:T(8,128)(2,1)} %param.12) | copy-start | bytes 9437188
  88.1 1.0 copy-start.3
  91.0 20.3 %all-to-all-start.2 = ((bf16[4,32,2,2,768]{4,1,3,2,0:T(8,128)(2,1)}), bf16[4,32,2,2,768]{4,1,3,2,0:T(8,128)(2,1)}, u32[]{:S(2)}, u32[]{:S(2)}) async-start(bf16[4,32,2,2,768]{4,1,3,2,0:T(8,128)(2,1)} %copy.42), calls=%async_computation.2 | async-start | bytes 1572864 | tf_op jit(solution)/shard_map/all_to_all | solution.py:55
  111.3 25.3 %all-to-all-start.1 = ((bf16[4,32,2,2,768]{4,1,3,2,0:T(8,128)(2,1)}), bf16[4,32,2,2,768]{4,1,3,2,0:T(8,128)(2,1)}, u32[]{:S(2)}, u32[]{:S(2)}) async-start(bf16[4,32,2,2,768]{4,1,3,2,0:T(8,128)(2,1)} %copy.41), calls=%async_computation.1 | async-start | bytes 1572864 | tf_op jit(solution)/shard_map/all_to_all | solution.py:55
  156.4 17.3 %copy-start.4 = (f32[12,8]{0,1:T(8,128)S(1)}, f32[12,8]{0,1:T(8,128)}, u32[]{:S(2)}) copy-start(f32[12,8]{0,1:T(8,128)} %param.10) | copy-start | bytes 1156
  158.2 70.8 %copy-start.2 = (bf16[12,4096]{1,0:T(8,128)(2,1)S(1)}, bf16[12,4096]{1,0:T(8,128)(2,1)}, u32[]{:S(2)}) copy-start(bf16[12,4096]{1,0:T(8,128)(2,1)} %copy-done.1) | copy-start | bytes 294916
  158.2 65.4 %all-to-all-start.3 = ((bf16[128,4,1024]{2,1,0:T(4,128)(2,1)}), bf16[128,4,1024]{2,1,0:T(4,128)(2,1)}, u32[]{:S(2)}, u32[]{:S(2)}) async-start(bf16[128,4,1024]{2,1,0:T(4,128)(2,1)} %copy.43), calls=%async_computation.3 | async-start | bytes 2097152 | tf_op jit(solution)/shard_map/all_to_all | solution.py:73
